TPU v7x, 32 devices: a whole 2x2x4 slice. The times are simulated.
32 devices in a mesh: dom: 8 (over y, x, core), sub: 4 (over z).
Axes of the slice: x: 2, y: 2, z: 4, core: 2. Of those that a mesh axis runs over, the one named last changes fastest.
Arguments:
- positions: bfloat16 [3, 4096], P(None, ('dom', 'sub')), may hold values from 0 to 1
- species: int32 [4096], P(('dom', 'sub')), may hold values from 0 to 1
- neighbours: int32 [64, 4096], P(None, ('dom', 'sub')), may hold values from -1 to 255, as said below
- ghost_rows: int32 [4, 1024], P(None, ('dom', 'sub')), may hold values from 0 to 127
- wavevectors: int32 [3, 12288], replicated, may hold values from -19 to 20, as said below
- embedding: bfloat16 [2, 128], replicated, may hold values from -6 to 6
- w_in: bfloat16 [2, 128, 128], replicated, may hold values from -0.5 to 0.5
- radial: bfloat16 [2, 8, 128], replicated, may hold values from -2 to 2
- norm_gain: bfloat16 [2, 128], replicated, may hold values from 0.25 to 1.75
- w_out: bfloat16 [2, 128, 128], replicated, may hold values from -0.5 to 0.5
- w_charge: bfloat16 [128, 8], replicated, may hold values from -0.5 to 0.5
Outputs:
- potentials: float32 [8, 4096], P(None, ('dom', 'sub'))
- forces: float32 [3, 4096], P(None, ('dom', 'sub'))
Inputs may be any that keep to these rules, and one draw needn't show every extreme that they name: `neighbours`: used slots come first in each atom's list, -1 fills the rest, and every list uses 64 // 2 slots or more; an entry below 128 is one of the device's own atoms, else it is ghost number (entry - 128) % 32 of block (entry - 128) // 32 of the table. `wavevectors`: the columns are distinct; the first nonzero component of each column is positive; the sum of the squares of a column is at most 400.
All inputs are finite; a program needn't handle non-finite values.
Results may differ from a plain program's by a relative error of at most 0.0067.
Values may be sent and summed in bfloat16 or wider, within the bound.
No kernel may reach another device: no remote copies, remote signals or barrier semaphores. Data moves between devices by JAX's collectives and lax.ppermute only.
A program may use at most 64 MiB of HBM per device.

v0:
```python
import math

import jax
import jax.numpy as jnp
from jax import lax
from jax.sharding import PartitionSpec as P

smearing = 0.005
epsilon = 1e-05
highest = lax.Precision.HIGHEST


def from_behind(value, axis, steps):
    count = lax.axis_size(axis)
    pairs = [(source, (source + steps) % count) for source in range(count)]
    return lax.ppermute(value, axis, pairs)


def swap_ghosts(outgoing):
    received = []
    for source, offset in ((1, 1), (0, -1)):
        received.append(from_behind(outgoing[source], "dom", offset))
    for source, offset in ((3, 1), (2, -1)):
        received.append(from_behind(outgoing[source], "sub", offset))
    return received


def phase_tile(wave_float, coords, first_k, block_len):
    chosen = lax.dynamic_slice_in_dim(wave_float, first_k, block_len, 1)
    angle = chosen[0][:, None] * coords[0][None, :] + chosen[1][:, None] * coords[1][None, :]
    angle = 2.0 * math.pi * (angle + chosen[2][:, None] * coords[2][None, :])
    return (chosen, jnp.concatenate([jnp.cos(angle), jnp.sin(angle)], axis=0))


def per_device(
    positions,
    species,
    neighbours,
    ghost_rows,
    wavevectors,
    embedding,
    w_in,
    radial,
    norm_gain,
    w_out,
    w_charge,
):
    atom_count = positions.shape[1]
    channels = w_in.shape[2]
    coords = positions.astype(jnp.float32)
    ghost_coords = swap_ghosts([positions[:, ghost_rows[side_number]] for side_number in range(4)])
    coord_table = jnp.concatenate([positions] + ghost_coords, axis=1).astype(jnp.float32)
    clamped = jnp.maximum(neighbours, 0)
    live_mask = (neighbours >= 0)[:, :, None]
    nearby = coord_table[:, clamped]
    displace = nearby - coords[:, None, :]
    chord_sq = jnp.sum(jnp.sin(math.pi * displace) ** 2, axis=0)
    decay_rates = jnp.exp2(jnp.arange(radial.shape[1], dtype=jnp.float32) - 3.0)
    radial_basis = jnp.exp(-decay_rates[:, None, None] * chord_sq[None, :, :])
    atom_block = math.gcd(atom_count, 256)
    hidden = jnp.where((species == 1)[:, None], embedding[1][None, :], embedding[0][None, :])
    for layer_number in range(w_in.shape[0]):
        projected = jnp.dot(hidden, w_in[layer_number], preferred_element_type=jnp.float32).astype(
            jnp.bfloat16
        )
        ghost_feats = swap_ghosts([projected[ghost_rows[side_number]] for side_number in range(4)])
        feat_table = jnp.concatenate([projected] + ghost_feats, axis=0)
        radial_layer = radial[layer_number].astype(jnp.float32)

        def message_block(block_number, message, feat_table=feat_table, radial_layer=radial_layer):
            edge_weight = jnp.einsum("bna,bc->nac", radial_basis, radial_layer, precision=highest)
            gathered = feat_table[clamped].astype(jnp.float32)
            part_sum = jnp.sum(jnp.where(live_mask, edge_weight * gathered, 0.0), axis=0)
            return part_sum

        message = lax.fori_loop(
            0,
            atom_count // atom_block,
            message_block,
            jnp.zeros((atom_count, channels), jnp.float32),
        )
        normed = message * lax.rsqrt(jnp.mean(message * message, axis=1, keepdims=True) + epsilon)
        normed = normed * norm_gain[layer_number].astype(jnp.float32)[None, :]
        activated = jax.nn.silu(normed).astype(jnp.bfloat16)
        update = jnp.dot(activated, w_out[layer_number], preferred_element_type=jnp.float32)
        hidden = (hidden.astype(jnp.float32) + update).astype(jnp.bfloat16)
    charges = jnp.dot(
        hidden.astype(jnp.float32),
        w_charge.astype(jnp.float32),
        precision=highest,
        preferred_element_type=jnp.float32,
    ).T
    latent = charges.shape[0]
    wave_float = wavevectors.astype(jnp.float32)
    total_k = wave_float.shape[1]
    block_len = math.gcd(total_k, 512)
    block_count = total_k // block_len
    squared = jnp.sum(wave_float * wave_float, axis=0)
    kweight = jnp.exp(-smearing * squared) / squared

    def accumulate(block_number, structure):
        first_k = block_number * block_len
        chosen, tile = phase_tile(wave_float, coords, first_k, block_len)
        piece = lax.dot_general(
            charges,
            tile,
            (((1,), (1,)), ((), ())),
            precision=highest,
            preferred_element_type=jnp.float32,
        )
        piece = jnp.concatenate([piece[:, :block_len], piece[:, block_len:]], axis=0)
        return lax.dynamic_update_slice_in_dim(structure, piece, first_k, 1)

    structure = lax.fori_loop(
        0, block_count, accumulate, jnp.zeros((2 * latent, total_k), jnp.float32)
    )
    weighted = lax.psum(structure, ("dom", "sub")) * kweight[None, :]

    def apply_block(block_number, carry):
        potential, force_sum = carry
        first_k = block_number * block_len
        chosen, tile = phase_tile(wave_float, coords, first_k, block_len)
        cos_weight = lax.dynamic_slice(weighted, (0, first_k), (latent, block_len))
        sin_weight = lax.dynamic_slice(weighted, (latent, first_k), (latent, block_len))
        force_left = jnp.concatenate(
            [
                -(chosen[:, None, :] * sin_weight[None, :, :]),
                chosen[:, None, :] * cos_weight[None, :, :],
            ],
            axis=2,
        )
        left_rows = jnp.concatenate(
            [
                jnp.concatenate([cos_weight, sin_weight], axis=1),
                force_left.reshape(3 * latent, 2 * block_len),
            ],
            axis=0,
        )
        product = jnp.dot(left_rows, tile, precision=highest, preferred_element_type=jnp.float32)
        potential = potential + product[:latent]
        inner_terms = product[latent:].reshape(3, latent, atom_count)
        force_sum = force_sum + jnp.sum(charges[None, :, :] * inner_terms, axis=1)
        return (potential, force_sum)

    start = (jnp.zeros((latent, atom_count), jnp.float32), jnp.zeros((3, atom_count), jnp.float32))
    potential, force_sum = lax.fori_loop(0, block_count, apply_block, start)
    scale = 1.0 / math.sqrt(atom_count * lax.axis_size(("dom", "sub")))
    return (potential * scale, force_sum * scale)


def solution(mesh):
    return jax.shard_map(
        per_device,
        mesh=mesh,
        in_specs=(
            P(None, ("dom", "sub")),
            P(("dom", "sub")),
            P(None, ("dom", "sub")),
            P(None, ("dom", "sub")),
            P(),
            P(),
            P(),
            P(),
            P(),
            P(),
            P(),
        ),
        out_specs=(P(None, ("dom", "sub")), P(None, ("dom", "sub"))),
        check_vma=False,
    )
```

profile of v0, /device:TPU:0, one launch (start us, length us, event | category | flops | bytes accessed | tf_op | source)
XLA Modules:
  0.0 366.5 jit_solution(11224052478974739942)
XLA Ops:
  12.2 2.9 collective-permute-start.5
  15.7 2.4 collective-permute-start.6
  20.1 2.7 collective-permute-start.1
  27.8 1.1 multiply_reduce_fusion
  28.9 1.6 collective-permute-start.2
  30.6 2.3 collective-permute-start.3
  32.9 1.4 collective-permute-done.2
  35.7 27.7 %gather_fusion.4 = f32[8192,3]{1,0:T(8,128)} fusion(f32[3,256]{0,1:T(8,128)S(1)} %copy.47, s32[8192]{0:T(1024)S(1)} %bitcast_clamp_fusion), kind=kCustom, calls=%fused_computation.4 | custom fusion | bytes 229376 | tf_op jit(solution)/shard_map/gather | solution.py:55
  63.4 2.8 copy.49
  66.6 5.1 %fusion.29 = f32[64,128,128]{2,1,0:T(8,128)} fusion(f32[64,128]{1,0:T(8,128)S(1)} %fusion.37, f32[8]{0:T(128)S(1)} %exponential_negate_fusion, bf16[2,8,128]{2,1,0:T(8,128)(2,1)S(1)} %copy-done.3), kind=kOutput, calls=%fused_computation.73 | convolution fusion | flops 100728832 | bytes 4229632 | tf_op jit(solution)/shard_map/while/body/eval_jaxpr/bna,bc->nac/dot_general | solution.py:71
  71.8 24.0 %gather_fusion.9 = bf16[8192,128]{1,0:T(8,128)(2,1)S(1)} fusion(bf16[256,128]{1,0:T(8,128)(2,1)S(1)} %constant_dynamic-update-slice_fusion, s32[8192]{0:T(1024)S(1)} %bitcast_clamp_fusion), kind=kCustom, calls=%fused_computation.9 | custom fusion | bytes 4227072 | tf_op jit(solution)/shard_map/while/body/eval_jaxpr/gather | solution.py:72
  95.9 3.7 %fusion.25 = f32[128,128]{1,0:T(8,128)S(1)} fusion(f32[64,128,128]{2,1,0:T(8,128)} %fusion.29, bf16[64,128,128]{2,1,0:T(8,128)(2,1)S(1)} %bitcast.132, pred[64,128]{1,0:T(8,128)(4,1)S(1)} %broadcast_compare_fusion), kind=kLoop, calls=%fused_computation.62 | loop fusion | flops 4177920 | bytes 6365184 | tf_op jit(solution)/shard_map/while/body/eval_jaxpr/reduce_sum | solution.py:73
  100.7 5.1 %fusion.28 = f32[64,128,128]{2,1,0:T(8,128)} fusion(f32[64,128]{1,0:T(8,128)S(1)} %fusion.37, f32[8]{0:T(128)S(1)} %exponential_negate_fusion, bf16[2,8,128]{2,1,0:T(8,128)(2,1)S(1)} %copy-done.3), kind=kOutput, calls=%fused_computation.72 | convolution fusion | flops 100728832 | bytes 4229632 | tf_op jit(solution)/shard_map/while/body/eval_jaxpr/bna,bc->nac/dot_general | solution.py:71
  107.6 2.7 collective-permute-start.9
  110.3 1.8 collective-permute-start.10
  112.1 2.0 collective-permute-start.11
  114.1 1.7 collective-permute-done.10
  115.8 24.0 %gather_fusion.14 = bf16[8192,128]{1,0:T(8,128)(2,1)S(1)} fusion(bf16[256,128]{1,0:T(8,128)(2,1)S(1)} %constant_dynamic-update-slice_fusion.5, s32[8192]{0:T(1024)S(1)} %bitcast_clamp_fusion), kind=kCustom, calls=%fused_computation.14 | custom fusion | bytes 4227072 | tf_op jit(solution)/shard_map/while/body/eval_jaxpr/gather | solution.py:72
  139.9 3.6 fusion.23
  144.1 41.6 %while.18 = (s32[]{:T(128)}, f32[16,12288]{1,0:T(8,128)S(1)}, f32[3,12288]{1,0:T(4,128)S(1)}, f32[3,128]{1,0:T(4,128)S(1)}, f32[8,128]{1,0:T(8,128)S(1)}, /*inde...) while((s32[]{:T(128)}, f32[16,12288]{1,0:T(8,128)S(1)}, f32[3,12288]{1,0:T(4,128)S(1)}, ...), condition=%wide.region_6.7_spmd, body=%wide.region_5.6_spmd.sunk | while | flops 13115400 | bytes 1239747 | solution.py:114
  184.0 1.0 fusion.82
  186.6 130.7 %all-reduce.2.cloned.1.call-done = f32[16,12288]{1,0:T(8,128)} async-done(((f32[16,12288]{1,0:T(8,128)}), f32[16,12288]{1,0:T(8,128)}) %all-reduce.2.cloned.1.call-update) | async-done | bytes 786448 | tf_op jit(solution)/shard_map/psum | solution.py:117
  317.3 1.2 broadcast_multiply_fusion
  318.5 40.0 %while.38 = (s32[]{:T(128)}, f32[8,128]{1,0:T(8,128)S(1)}, f32[3,128]{1,0:T(4,128)S(1)}, f32[16,12288]{1,0:T(8,128)S(1)}, f32[3,12288]{1,0:T(4,128)S(1)}, /*inde...) while((s32[]{:T(128)}, f32[8,128]{1,0:T(8,128)S(1)}, ...), condition=%wide.region_11.12_spmd.clone, body=%wide.region_9.11_spmd.clone.sunk | while | flops 50999688 | bytes 1469154 | solution.py:146
  (464 shorter events, 97.8 us)
Async XLA Ops:
  7.2 136.7 %copy-start = (bf16[128,8]{0,1:T(8,128)(2,1)S(1)}, bf16[128,8]{0,1:T(8,128)(2,1)}, u32[]{:S(2)}) copy-start(bf16[128,8]{0,1:T(8,128)(2,1)} %param.25) | copy-start | bytes 6148
  7.2 59.4 %copy-start.3 = (bf16[2,8,128]{2,1,0:T(8,128)(2,1)S(1)}, bf16[2,8,128]{2,1,0:T(8,128)(2,1)}, u32[]{:S(2)}) copy-start(bf16[2,8,128]{2,1,0:T(8,128)(2,1)} %param.22) | copy-start | bytes 12292
  7.2 310.1 %all-reduce.2.cloned.1.call-start = ((), (), s32[]{:S(2)}) async-start(), calls=%async_computation | async-start | bytes 1572864 | tf_op jit(solution)/shard_map/psum | solution.py:117
  11.0 60.7 %collective-permute-start.4 = (bf16[32,128]{1,0:T(8,128)(2,1)S(1)}, bf16[32,128]{1,0:T(8,128)(2,1)S(1)}, u32[]{:S(2)}, u32[]{:S(2)}) collective-permute-start(bf16[32,128]{1,0:T(8,128)(2,1)S(1)} %gather_fusion.5), channel_id=1, source_target_pairs={{0,4},{4,8},{8,12},{12,16},{16,20},{20,24},{24,28},{28,0},{1,5},{5... | collective-permute-start | bytes 24584 | tf_op jit(solution)/shard_map/ppermute | solution.py:16
  12.2 59.6 %collective-permute-start.5 = (bf16[32,128]{1,0:T(8,128)(2,1)S(1)}, bf16[32,128]{1,0:T(8,128)(2,1)S(1)}, u32[]{:S(2)}, u32[]{:S(2)}) collective-permute-start(bf16[32,128]{1,0:T(8,128)(2,1)S(1)} %gather_fusion.6), channel_id=1, source_target_pairs={{0,28},{4,0},{8,4},{12,8},{16,12},{20,16},{24,20},{28,24},{1,29},{... | collective-permute-start | bytes 24584 | tf_op jit(solution)/shard_map/ppermute | solution.py:16
  15.7 56.1 %collective-permute-start.6 = (bf16[32,128]{1,0:T(8,128)(2,1)S(1)}, bf16[32,128]{1,0:T(8,128)(2,1)S(1)}, u32[]{:S(2)}, u32[]{:S(2)}) collective-permute-start(bf16[32,128]{1,0:T(8,128)(2,1)S(1)} %gather_fusion.7), channel_id=1, source_target_pairs={{0,1},{1,2},{2,3},{3,0},{4,5},{5,6},{6,7},{7,4},{8,9},{9,10},{10,1... | collective-permute-start | bytes 24584 | tf_op jit(solution)/shard_map/ppermute | solution.py:16
  19.5 9.4 %collective-permute-start = (bf16[3,32]{0,1:T(8,128)(2,1)S(1)}, bf16[3,32]{0,1:T(8,128)(2,1)S(1)}, u32[]{:S(2)}, u32[]{:S(2)}) collective-permute-start(bf16[3,32]{0,1:T(8,128)(2,1)S(1)} %bitcast.143), channel_id=1, source_target_pairs={{0,4},{4,8},{8,12},{12,16},{16,20},{20,24},{24,28},{28,0},{1,5},{5... | collective-permute-start | bytes 584 | tf_op jit(solution)/shard_map/ppermute | solution.py:16
  20.1 10.5 %collective-permute-start.1 = (bf16[3,32]{0,1:T(8,128)(2,1)S(1)}, bf16[3,32]{0,1:T(8,128)(2,1)S(1)}, u32[]{:S(2)}, u32[]{:S(2)}) collective-permute-start(bf16[3,32]{0,1:T(8,128)(2,1)S(1)} %bitcast.142), channel_id=1, source_target_pairs={{0,28},{4,0},{8,4},{12,8},{16,12},{20,16},{24,20},{28,24},{1,29},{... | collective-permute-start | bytes 584 | tf_op jit(solution)/shard_map/ppermute | solution.py:16
  28.9 5.5 %collective-permute-start.2 = (bf16[3,32]{0,1:T(8,128)(2,1)S(1)}, bf16[3,32]{0,1:T(8,128)(2,1)S(1)}, u32[]{:S(2)}, u32[]{:S(2)}) collective-permute-start(bf16[3,32]{0,1:T(8,128)(2,1)S(1)} %bitcast.141), channel_id=1, source_target_pairs={{0,1},{1,2},{2,3},{3,0},{4,5},{5,6},{6,7},{7,4},{8,9},{9,10},{10,1... | collective-permute-start | bytes 584 | tf_op jit(solution)/shard_map/ppermute | solution.py:16
  30.6 4.1 %collective-permute-start.3 = (bf16[3,32]{0,1:T(8,128)(2,1)S(1)}, bf16[3,32]{0,1:T(8,128)(2,1)S(1)}, u32[]{:S(2)}, u32[]{:S(2)}) collective-permute-start(bf16[3,32]{0,1:T(8,128)(2,1)S(1)} %bitcast.140), channel_id=1, source_target_pairs={{0,3},{1,0},{2,1},{3,2},{4,7},{5,4},{6,5},{7,6},{8,11},{9,8},{10,9... | collective-permute-start | bytes 584 | tf_op jit(solution)/shard_map/ppermute | solution.py:16
  34.4 37.4 %collective-permute-start.7 = (bf16[32,128]{1,0:T(8,128)(2,1)S(1)}, bf16[32,128]{1,0:T(8,128)(2,1)S(1)}, u32[]{:S(2)}, u32[]{:S(2)}) collective-permute-start(bf16[32,128]{1,0:T(8,128)(2,1)S(1)} %gather_fusion.8), channel_id=1, source_target_pairs={{0,3},{1,0},{2,1},{3,2},{4,7},{5,4},{6,5},{7,6},{8,11},{9,8},{10,9... | collective-permute-start | bytes 24584 | tf_op jit(solution)/shard_map/ppermute | solution.py:16
  95.9 3.8 %copy-start.4 = (bf16[2,128,128]{2,1,0:T(8,128)(2,1)S(1)}, bf16[2,128,128]{2,1,0:T(8,128)(2,1)}, u32[]{:S(2)}) copy-start(bf16[2,128,128]{2,1,0:T(8,128)(2,1)} %param.24) | copy-start | bytes 196612
  95.9 4.0 %copy-start.2 = (bf16[2,128,128]{2,1,0:T(8,128)(2,1)S(1)}, bf16[2,128,128]{2,1,0:T(8,128)(2,1)}, u32[]{:S(2)}) copy-start(bf16[2,128,128]{2,1,0:T(8,128)(2,1)} %param.21) | copy-start | bytes 196612
  100.7 13.4 %collective-permute-start.8 = (bf16[32,128]{1,0:T(8,128)(2,1)S(1)}, bf16[32,128]{1,0:T(8,128)(2,1)S(1)}, u32[]{:S(2)}, u32[]{:S(2)}) collective-permute-start(bf16[32,128]{1,0:T(8,128)(2,1)S(1)} %gather_fusion.10), channel_id=1, source_target_pairs={{0,4},{4,8},{8,12},{12,16},{16,20},{20,24},{24,28},{28,0},{1,5},{5... | collective-permute-start | bytes 24584 | tf_op jit(solution)/shard_map/ppermute | solution.py:16
  107.6 6.5 %collective-permute-start.9 = (bf16[32,128]{1,0:T(8,128)(2,1)S(1)}, bf16[32,128]{1,0:T(8,128)(2,1)S(1)}, u32[]{:S(2)}, u32[]{:S(2)}) collective-permute-start(bf16[32,128]{1,0:T(8,128)(2,1)S(1)} %gather_fusion.11), channel_id=1, source_target_pairs={{0,28},{4,0},{8,4},{12,8},{16,12},{20,16},{24,20},{28,24},{1,29},{... | collective-permute-start | bytes 24584 | tf_op jit(solution)/shard_map/ppermute | solution.py:16
  110.3 5.5 %collective-permute-start.10 = (bf16[32,128]{1,0:T(8,128)(2,1)S(1)}, bf16[32,128]{1,0:T(8,128)(2,1)S(1)}, u32[]{:S(2)}, u32[]{:S(2)}) collective-permute-start(bf16[32,128]{1,0:T(8,128)(2,1)S(1)} %gather_fusion.12), channel_id=1, source_target_pairs={{0,1},{1,2},{2,3},{3,0},{4,5},{5,6},{6,7},{7,4},{8,9},{9,10},{10,1... | collective-permute-start | bytes 24584 | tf_op jit(solution)/shard_map/ppermute | solution.py:16
  112.1 3.8 %collective-permute-start.11 = (bf16[32,128]{1,0:T(8,128)(2,1)S(1)}, bf16[32,128]{1,0:T(8,128)(2,1)S(1)}, u32[]{:S(2)}, u32[]{:S(2)}) collective-permute-start(bf16[32,128]{1,0:T(8,128)(2,1)S(1)} %gather_fusion.13), channel_id=1, source_target_pairs={{0,3},{1,0},{2,1},{3,2},{4,7},{5,4},{6,5},{7,6},{8,11},{9,8},{10,9... | collective-permute-start | bytes 24584 | tf_op jit(solution)/shard_map/ppermute | solution.py:16
  185.6 0.9 copy-start.1
Sparse Core Ops, SparseCore 0:
  186.7 130.5 all-reduce.1
where the time goes:
time: 367 us
  waiting for transfers between devices  134 us (37%)
  local copies, waits for them, and re-layouts  93.8 us (26%)
  other arithmetic  68.1 us (19%)
  matrix products  34.4 us (9%)
  starting transfers between devices  19.3 us (5%)
  between operations  14.3 us (4%)
    psum x1, waiting for transfers between devices, per_device(): weighted = lax.psum(structure, ('dom', 'sub')) * kweight[None, :]  131 us
    cos x48, other arithmetic, phase_tile(): return (chosen, jnp.concatenate([jnp.cos(angle), jnp.sin(angle)], axis=0))  49.8 us
    gather x2, local copies, waits for them, and re-layouts, message_block(): gathered = feat_table[clamped].astype(jnp.float32)  48 us
    gather x2, local copies, waits for them, and re-layouts, per_device(): nearby = coord_table[:, clamped]  30.5 us
    ppermute x12, starting transfers between devices, from_behind(): return lax.ppermute(value, axis, pairs)  19.2 us
    dot_general x24, matrix products, accumulate(): lax.dot_general(charges, tile, (((1,), (1,)), ((), ())), precision=highes...  13.1 us
    dot_general x2, matrix products, message_block(): jnp.einsum('bna,bc->nac', radial_basis, radial_layer, precision=highest)  10.2 us
    dot_general x24, matrix products, apply_block(): jnp.dot(left_rows, tile, precision=highest, preferred_element_type=jnp.fl...  9.39 us
  transfers between devices with their start and end apart: 13, of which 3 were waited for; matrix products, arithmetic and copies ran while one was open for 15% of the time, Pallas kernels for 0%

commit v1 on v0

v1 whole, which is shorter than its diff:
```python
import functools
import math

import jax
import jax.numpy as jnp
from jax import lax
from jax.experimental import pallas as pl
from jax.experimental.pallas import tpu as pltpu
from jax.sharding import PartitionSpec as P

f32, bf16, i32 = jnp.float32, jnp.bfloat16, jnp.int32
smearing = 0.005
epsilon = 1e-05
highest = lax.Precision.HIGHEST

reach = 20
harmonics = reach + 1
signed = 2 * reach
pair_groups = 48
pairs = 8 * pair_groups
lane_blocks = pairs // 128
mask_rows = lane_blocks * 2 * signed
common = 8

sin_terms = (3.14159258, -5.16770688, 2.55003138, -0.59804517, 0.07722013)
cos_terms = (0.99999995, -4.93479286, 4.05841191, -1.33188016, 0.21969679)
sends = ((1, 0), (-1, 0), (0, 1), (0, -1))
ghost_order = (1, 0, 3, 2)


def poly(terms, square):
    total = jnp.full_like(square, terms[-1])
    for term in terms[-2::-1]:
        total = total * square + term
    return total


def sin_pi(turns):
    rest = turns - jnp.round(turns)
    return rest * poly(sin_terms, rest * rest)


def cos_sin(turns):
    rest = turns - jnp.round(turns)
    square = rest * rest
    half_sin = rest * poly(sin_terms, square)
    half_cos = poly(cos_terms, square)
    return 1.0 - 2.0 * half_sin * half_sin, 2.0 * half_sin * half_cos


def iota(shape, axis):
    return lax.broadcasted_iota(i32, shape, axis)


def lanes_of(shape, width):
    return lax.div(iota(shape, len(shape) - 1), jnp.int32(width))


def by_block(parts, width):
    which = lanes_of(parts[0].shape, width)
    out = parts[-1]
    for number in range(len(parts) - 2, -1, -1):
        out = jnp.where(which == number, parts[number], out)
    return out


def row_of(values, row, count):
    return jnp.broadcast_to(values[row : row + 1], (count,) + values.shape[1:])


def take_lanes(row_values, index):
    return jnp.take_along_axis(row_values, index, axis=1)


def dot(left, right, dims, precision=None):
    return lax.dot_general(left, right, ((dims[0], dims[1]), ((), ())), precision=precision, preferred_element_type=f32)


def pack_kernel(sizes, pos_ref, spec_ref, nbr_ref, rows_ref, out_ref):
    n_dom, n_sub = sizes
    count, _, atoms = out_ref.shape
    ghosts = rows_ref.shape[1]
    slots = nbr_ref.shape[0]
    quarter = slots // 4
    order = jnp.concatenate([rows_ref[row : row + 1, :] for row in ghost_order], axis=1)
    head = jnp.concatenate(
        [
            pos_ref[...].astype(f32),
            spec_ref[...].astype(f32),
            order.astype(f32),
            jnp.zeros((common - 5, atoms), f32),
        ],
        axis=0,
    )
    whole = jnp.concatenate([head, jnp.zeros((quarter, atoms), f32)], axis=0).astype(bf16)
    for device in range(count):
        out_ref[device] = whole
    index = jnp.broadcast_to(order, (8, atoms))
    lists = [take_lanes(nbr_ref[8 * s : 8 * s + 8, :], index).astype(f32) for s in range(slots // 8)]
    per = quarter // 8
    dom, sub = lax.axis_index("dom"), lax.axis_index("sub")
    for block, (dom_step, sub_step) in enumerate(sends):
        rows = []
        for piece in range(per):
            parts = [
                pltpu.roll(lists[r * per + piece], (ghosts * (r - block)) % atoms, 1) if r != block else lists[r * per + piece]
                for r in range(4)
            ]
            rows.append(by_block(parts, ghosts))
        target = lax.rem(dom + dom_step + n_dom, n_dom) * n_sub + lax.rem(sub + sub_step + n_sub, n_sub)
        out_ref[target, common:, :] = jnp.concatenate(rows, axis=0).astype(bf16)


def first_layer_sums(lists, tables, centre, ghosts, bases):
    total = [[None] * bases for _ in range(2)]
    for listed in lists:
        index = jnp.maximum(listed, 0)
        low = jnp.bitwise_and(index, 127)
        is_ghost = index >= 128
        found = []
        for quantity in range(4):
            parts = [
                jnp.where(is_ghost, take_lanes(row_of(outer, quantity, 8), low), take_lanes(row_of(inner, quantity, 8), low))
                for inner, outer in tables
            ]
            found.append(by_block(parts, ghosts) if len(parts) > 1 else parts[0])
        chord = jnp.zeros(low.shape, f32)
        for axis in range(3):
            wave = sin_pi(found[axis] - row_of(centre, axis, 8))
            chord = chord + wave * wave
        first = jnp.where(listed >= 0, jnp.exp(-0.125 * chord), 0.0)
        for kind in range(2):
            power = jnp.where((found[3] > 0.5) if kind else (found[3] <= 0.5), first, 0.0)
            for basis in range(bases):
                if basis:
                    power = power * power
                total[kind][basis] = power if total[kind][basis] is None else total[kind][basis] + power
    return jnp.concatenate(total[0] + total[1], axis=0)


def wave_mask(wave_ref, rows, device):
    first = wave_ref[0:1, :]
    second = wave_ref[1:2, :]
    third = wave_ref[2:3, :]
    size = jnp.abs(second)
    pair = jnp.where(
        size < 8,
        8 * first + size,
        jnp.where(size < 16, 160 + 8 * first + size, jnp.where(size < 20, 304 + 4 * first + size, 376)),
    )
    side = jnp.where(second < 0, 1, 0)
    block = jnp.right_shift(pair, 7)
    lane = jnp.bitwise_and(pair, 127)
    row = (block * 2 + side) * signed + third + (reach - 1) - device * rows
    inside = (row >= 0) & (row < rows)
    key = jnp.where(inside, jnp.right_shift(lane, 5) * rows + row, -1)
    low = jnp.bitwise_and(lane, 31)
    total_k = key.shape[1]
    left = jnp.where(iota((4 * rows, total_k), 0) == key, 1.0, 0.0).astype(bf16)
    right = jnp.where(iota((32, total_k), 0) == low, 1.0, 0.0).astype(bf16)
    found = dot(left, right, ((1,), (1,)))
    spread = jnp.concatenate([found] * 4, axis=1)
    return by_block([spread[q * rows : (q + 1) * rows] for q in range(4)], 32)


def normed_silu(message, gain):
    normed = message * lax.rsqrt(jnp.mean(message * message, axis=0, keepdims=True) + epsilon) * gain
    return (normed / (1.0 + jnp.exp(-normed))).astype(bf16)


def charge_kernel(
    sizes,
    cells,
    recv_ref,
    nbr_ref,
    wave_ref,
    emb_ref,
    w_in_ref,
    radial_ref,
    gain_ref,
    w_out_ref,
    w_charge_ref,
    out_ref,
    charge_ref,
):
    n_dom, n_sub = sizes
    count = out_ref.shape[0]
    atoms = nbr_ref.shape[1]
    slots = nbr_ref.shape[0]
    bases = radial_ref.shape[1]
    channels = w_in_ref.shape[1]
    ghosts = atoms // 4
    quarter = slots // 4
    dom, sub = lax.axis_index("dom"), lax.axis_index("sub")

    def device_at(dom_step, sub_step):
        return lax.rem(dom + dom_step + 2 * n_dom, n_dom) * n_sub + lax.rem(sub + sub_step + 2 * n_sub, n_sub)

    origins = tuple((-dom_step, -sub_step) for dom_step, sub_step in sends)
    data, picked = {}, {}
    for base in ((0, 0),) + origins:
        for step in ((0, 0),) + origins:
            key = (base[0] + step[0], base[1] + step[1])
            if key not in data:
                data[key] = recv_ref[device_at(*key), 0:common, :].astype(f32)
                index = row_of(data[key], 4, common).astype(i32)
                picked[key] = take_lanes(data[key], index)

    def table(key):
        return data[key], by_block([picked[(key[0] + s[0], key[1] + s[1])] for s in origins], ghosts)

    own = data[(0, 0)]
    own_table = table((0, 0))
    own_ghosts = own_table[1]

    own_lists = [nbr_ref[8 * s : 8 * s + 8, :] for s in range(slots // 8)]
    sent = [recv_ref[device_at(*key), common:, :].astype(f32) for key in origins]
    ghost_lists = []
    for r in range(4):
        for piece in range(quarter // 8):
            parts = []
            for block in range(4):
                part = sent[block][8 * piece : 8 * piece + 8]
                shift = (ghosts * (block - r)) % atoms
                parts.append(pltpu.roll(part, shift, 1) if shift else part)
            ghost_lists.append(by_block(parts, ghosts).astype(i32))

    sums = jnp.concatenate(
        [
            first_layer_sums(own_lists, [own_table], own, ghosts, bases),
            first_layer_sums(ghost_lists, [table(key) for key in origins], own_ghosts, ghosts, bases),
        ],
        axis=1,
    )
    kinds = jnp.concatenate([emb_ref[...].astype(f32), jnp.zeros((6, channels), f32)], axis=0).astype(bf16)
    two_feats = dot(kinds, w_in_ref[0], ((1,), (0,))).astype(bf16).astype(f32)
    radial_first = radial_ref[0].astype(f32)
    weights = jnp.concatenate(
        [
            jnp.broadcast_to(radial_first[basis : basis + 1] * two_feats[kind : kind + 1], (8, channels))
            for kind in range(2)
            for basis in range(bases)
        ],
        axis=0,
    )
    message = dot(weights, sums, ((0,), (0,)), highest)

    params = jnp.concatenate(
        [radial_ref[1].astype(f32), gain_ref[...].astype(f32), jnp.zeros((16 - bases - 2, channels), f32)], axis=0
    ).astype(bf16)
    spread = jnp.where(iota((16, 16 * atoms), 0) == lanes_of((16, 16 * atoms), atoms), 1.0, 0.0).astype(bf16)
    columns = dot(params, spread, ((0,), (0,)))

    def column(number):
        return columns[:, number * atoms : (number + 1) * atoms]

    gain_first = column(bases)
    activated = normed_silu(message, jnp.concatenate([gain_first, gain_first], axis=1))
    species = jnp.concatenate([own[3:4], own_ghosts[3:4]], axis=1)
    kind_rows = iota((8, 2 * atoms), 0)
    choice = jnp.where((kind_rows < 2) & (jnp.where(species > 0.5, 1, 0) == kind_rows), 1.0, 0.0).astype(bf16)
    hidden = dot(kinds, choice, ((0,), (0,)))
    hidden = (hidden + dot(w_out_ref[0], activated, ((0,), (0,)))).astype(bf16)
    feats = dot(w_in_ref[1], hidden, ((0,), (0,))).astype(bf16)

    near = [cos_sin(jnp.concatenate([own, own_ghosts], axis=1))]
    is_axis = iota((8, 2 * atoms), 0) < 3
    cosines = jnp.where(is_axis, near[0][0], 0.0)
    sines = jnp.where(is_axis, near[0][1], 0.0)
    waves = jnp.concatenate([cosines, sines], axis=0)
    chord = 1.5 - 0.5 * dot(waves, waves[:, :atoms], ((0,), (0,)), highest)
    listed = [nbr_ref[8 * s : 8 * s + 8, :].astype(f32) for s in range(slots // 8)]
    halves = []
    for half in range(2):
        row_number = (iota((atoms, atoms), 0) + half * atoms).astype(f32)
        times = jnp.zeros((atoms, atoms), f32)
        for slot in range(slots):
            times = times + jnp.where(row_number == row_of(listed[slot // 8], slot % 8, atoms), 1.0, 0.0)
        halves.append(times)
    times = jnp.concatenate(halves, axis=0)
    power = jnp.exp(-0.125 * chord)
    message = jnp.zeros((channels, atoms), f32)
    for basis in range(bases):
        if basis:
            power = power * power
        weighted = times * power
        high = weighted.astype(bf16)
        low = (weighted - high.astype(f32)).astype(bf16)
        mixed = dot(feats, high, ((1,), (0,))) + dot(feats, low, ((1,), (0,)))
        message = message + column(basis) * mixed
    activated = normed_silu(message, column(bases + 1))
    hidden = (hidden[:, :atoms].astype(f32) + dot(w_out_ref[1], activated, ((0,), (0,)))).astype(bf16)
    charges = dot(w_charge_ref[...], hidden, ((0,), (0,)))
    charge_ref[...] = charges
    mask = wave_mask(wave_ref, cells, dom * n_sub + sub)
    fill = out_ref.shape[1] - charges.shape[0] - cells
    pieces = [charges, mask] + ([jnp.zeros((fill, atoms), f32)] if fill else [])
    block = jnp.concatenate(pieces, axis=0).astype(bf16)
    for device in range(count):
        out_ref[device] = block


def harmonic_tables(coords):
    lanes = coords.shape[1]
    step = iota((8, lanes), 0)
    big = jnp.where(step < 3, 8.0, 16.0)
    far = jnp.concatenate([coords[0:3], coords[0:3], coords[0:2]], axis=0)
    jump_cos, jump_sin = cos_sin(big * far)
    tables = []
    for axis in range(3):
        cos_low, sin_low = cos_sin(step.astype(f32) * row_of(coords, axis, 8))
        cosines, sines = [cos_low], [sin_low]
        for jump in (axis, 3 + axis):
            c, s = row_of(jump_cos, jump, 8), row_of(jump_sin, jump, 8)
            cosines.append(cos_low * c - sin_low * s)
            sines.append(sin_low * c + cos_low * s)
        tables.append((cosines, sines))
    return tables


def pair_rows(first, second):
    lanes = first[0].shape[1]
    lower = iota((8, lanes), 0) < 4

    def of(number):
        return row_of(first[number // 8], number % 8, 8)

    groups = [of(h) * second[0] for h in range(21)]
    groups += [of(h) * second[1] for h in range(19)]
    swapped = pltpu.roll(second[2], 4, 0)
    tail = jnp.where(lower, second[2], swapped)
    groups += [jnp.where(lower, of(2 * g), of(2 * g + 1)) * tail for g in range(7)]
    groups.append(of(0) * swapped)
    return groups


def pair_values(numbers):
    tail = numbers - 320
    first = jnp.where(
        numbers < 168,
        jnp.right_shift(numbers, 3),
        jnp.where(numbers < 320, jnp.right_shift(numbers - 168, 3), jnp.where(numbers < 376, jnp.right_shift(tail, 2), 0)),
    )
    second = jnp.where(
        numbers < 168,
        jnp.bitwise_and(numbers, 7),
        jnp.where(
            numbers < 320, jnp.bitwise_and(numbers, 7) + 8, jnp.where(numbers < 376, jnp.bitwise_and(tail, 3) + 16, 20)
        ),
    )
    return first, second


def ewald_kernel(sizes, cells, total_atoms, recv_ref, sum_ref, charge_ref, pos_ref, pot_ref, force_ref, grid_ref, left_ref, prod_ref, mask_ref, mix_ref):
    n_dom, n_sub = sizes
    latent, atoms = charge_ref.shape
    count = recv_ref.shape[0]
    chunk = grid_ref.shape[1] // atoms
    rows = latent * 2 * harmonics

    def build(device, place):
        coords = recv_ref[device, 0:common, :].astype(f32)
        tables = harmonic_tables(coords)
        spot = pl.ds(pl.multiple_of(place * atoms, atoms), atoms)
        charge = sum_ref[device, 0:latent, :].astype(f32)
        left = []
        for kind in range(2):
            left += [charge * row_of(tables[2][kind][m // 8], m % 8, latent) for m in range(harmonics)]
        for at in range(0, 2 * harmonics, 2):
            left_ref[at * latent : (at + 2) * latent, spot] = jnp.concatenate(left[at : at + 2], axis=0).astype(bf16)
        for kind in range(4):
            groups = pair_rows(tables[0][kind // 2], tables[1][kind % 2])
            for at in range(0, pair_groups, 2):
                start = kind * pairs + at * 8
                grid_ref[start : start + 16, spot] = jnp.concatenate(groups[at : at + 2], axis=0).astype(bf16)

    def whole_chunk(number, carry):
        def one(place, inner):
            build(number * chunk + place, place)
            return inner

        lax.fori_loop(0, chunk, one, 0)

        def tile(column, inner):
            spot = pl.ds(pl.multiple_of(column * 256, 256), 256)
            part = dot(left_ref[...], grid_ref[spot, :], ((1,), (1,)))

            @pl.when(number == 0)
            def _():
                prod_ref[:, spot] = part

            @pl.when(number > 0)
            def _():
                prod_ref[:, spot] = prod_ref[:, spot] + part

            return inner

        return lax.fori_loop(0, 4 * pairs // 256, tile, carry)

    lax.fori_loop(0, count // chunk, whole_chunk, 0)

    for device in range(-(-mask_rows // cells)):
        mask_ref[device * cells : (device + 1) * cells, :] = sum_ref[device, latent : latent + cells, :].astype(f32)
    first, second = pair_values(iota((8, pairs), 1))
    flat = (first * first + second * second).astype(f32)
    for m in range(harmonics):
        square = flat + float(m * m)
        square = jnp.maximum(square, 1.0)
        decay = jnp.exp(-smearing * square) / square
        for block in range(lane_blocks):
            factor = decay[:, block * 128 : (block + 1) * 128]

            def cell(side, third):
                row = (block * 2 + side) * signed + third + reach - 1
                return jnp.broadcast_to(mask_ref[row : row + 1, :], (8, 128)) * factor

            up = [cell(side, m) for side in range(2)]
            if 0 < m < reach:
                down = [cell(side, -m) for side in range(2)]
                upper = [up[side] + down[side] for side in range(2)]
                lower = [up[side] - down[side] for side in range(2)]
            else:
                upper = lower = up
            weight = (upper[0] + upper[1], upper[0] - upper[1], lower[0] + lower[1], lower[0] - lower[1])

            def at(u, v, w):
                row = (u * harmonics + m) * latent
                col = (v * 2 + w) * pairs + block * 128
                return slice(row, row + latent), slice(col, col + 128)

            real = (at(0, 0, 0), at(0, 1, 1), at(1, 1, 0), at(1, 0, 1))
            imag = (at(0, 1, 0), at(0, 0, 1), at(1, 0, 0), at(1, 1, 1))
            for places, signs in ((real, (1, -1, -1, -1)), (imag, (1, 1, 1, -1))):
                values = [prod_ref[place] for place in places]
                for j, place in enumerate(places):
                    mixed = None
                    for i, value in enumerate(values):
                        term = weight[i ^ j] * value
                        if mixed is None:
                            mixed = term if signs[i] == signs[j] else -term
                        else:
                            mixed = mixed + term if signs[i] == signs[j] else mixed - term
                    mix_ref[place] = mixed

    coords = jnp.concatenate([pos_ref[...].astype(f32), jnp.zeros((5, atoms), f32)], axis=0)
    tables = harmonic_tables(coords)
    first, second = pair_values(iota((pairs, atoms), 0))
    first, second = first.astype(f32), second.astype(f32)
    basis = [jnp.concatenate(pair_rows(tables[0][kind // 2], tables[1][kind % 2]), axis=0) for kind in range(4)]
    along_x = [-first * basis[2], -first * basis[3], first * basis[0], first * basis[1]]
    along_y = [-second * basis[1], second * basis[0], -second * basis[3], second * basis[2]]
    right = jnp.concatenate(
        [jnp.concatenate(part, axis=0).astype(bf16) for part in (basis, along_x, along_y)], axis=1
    )
    product = dot(mix_ref[...].astype(bf16), right, ((1,), (0,)))
    potential = jnp.zeros((latent, atoms), f32)
    slopes = [jnp.zeros((latent, atoms), f32) for _ in range(3)]
    for u in range(2):
        for m in range(harmonics):
            factor = row_of(tables[2][u][m // 8], m % 8, latent)
            turned = row_of(tables[2][1 - u][m // 8], m % 8, latent) * float(m if u else -m)
            row = (u * harmonics + m) * latent
            part = [product[row : row + latent, d * atoms : (d + 1) * atoms] for d in range(3)]
            potential = potential + factor * part[0]
            slopes[0] = slopes[0] + factor * part[1]
            slopes[1] = slopes[1] + factor * part[2]
            slopes[2] = slopes[2] + turned * part[0]
    scale = 1.0 / math.sqrt(total_atoms)
    pot_ref[...] = potential * scale
    charge = charge_ref[...]
    for d in range(3):
        force_ref[d : d + 1, :] = jnp.sum(charge * slopes[d], axis=0, keepdims=True) * -scale


def vmem(count):
    return [pl.BlockSpec(memory_space=pltpu.VMEM)] * count


def per_device(
    positions,
    species,
    neighbours,
    ghost_rows,
    wavevectors,
    embedding,
    w_in,
    radial,
    norm_gain,
    w_out,
    w_charge,
):
    axes = ("dom", "sub")
    sizes = (lax.axis_size("dom"), lax.axis_size("sub"))
    count = sizes[0] * sizes[1]
    atoms = positions.shape[1]
    latent = w_charge.shape[1]
    slots = neighbours.shape[0]
    outgoing = pl.pallas_call(
        functools.partial(pack_kernel, sizes),
        out_shape=jax.ShapeDtypeStruct((count, common + slots // 4, atoms), bf16),
        in_specs=vmem(4),
        out_specs=vmem(1)[0],
    )(positions, species[None, :], neighbours, ghost_rows)
    received = lax.all_to_all(outgoing, axes, 0, 0, tiled=True)
    cells = -(-mask_rows // count)
    rows_out = -(-(latent + cells) // 8) * 8
    outgoing, charges = pl.pallas_call(
        functools.partial(charge_kernel, sizes, cells),
        out_shape=(
            jax.ShapeDtypeStruct((count, rows_out, atoms), bf16),
            jax.ShapeDtypeStruct((latent, atoms), f32),
        ),
        in_specs=vmem(9),
        out_specs=tuple(vmem(2)),
    )(received, neighbours, wavevectors, embedding, w_in, radial, norm_gain, w_out, w_charge)
    sums = lax.all_to_all(outgoing, axes, 0, 0, tiled=True)
    chunk = math.gcd(count, 32)
    rows = latent * 2 * harmonics
    return pl.pallas_call(
        functools.partial(ewald_kernel, sizes, cells, atoms * count),
        out_shape=(
            jax.ShapeDtypeStruct((latent, atoms), f32),
            jax.ShapeDtypeStruct((3, atoms), f32),
        ),
        in_specs=vmem(4),
        out_specs=tuple(vmem(2)),
        scratch_shapes=[
            pltpu.VMEM((4 * pairs, chunk * atoms), bf16),
            pltpu.VMEM((rows, chunk * atoms), bf16),
            pltpu.VMEM((rows, 4 * pairs), f32),
            pltpu.VMEM((-(-mask_rows // cells) * cells, 128), f32),
            pltpu.VMEM((rows, 4 * pairs), f32),
        ],
    )(received, sums, charges, positions)


def solution(mesh):
    split = P(None, ("dom", "sub"))
    return jax.shard_map(
        per_device,
        mesh=mesh,
        in_specs=(split, P(("dom", "sub")), split, split) + (P(),) * 7,
        out_specs=(split, split),
        check_vma=False,
    )
```

time: 367 us -> 50.7 us (0.14)
  waiting for transfers between devices: 134 us -> 8.56 us
  local copies, waits for them, and re-layouts: 93.8 us -> 1.41 us
  other arithmetic: 68.1 us -> 0 us
  matrix products: 34.4 us -> 0 us
  Pallas kernels: 0 us -> 20.8 us
  between operations: 14.3 us -> 0.65 us
  starting transfers between devices: 19.3 us -> 7.33 us
  blocking collectives: 0 us -> 11.6 us
    psum x1 -> x0, waiting for transfers between devices: 131 us -> none  [per_device(): weighted = lax.psum(structure, ('dom', 'sub')) * kweight[None, :]]
    gather x16 -> x0, local copies, waits for them, and re-layouts: 85.7 us -> none  [the longest x2 48 us: message_block(): gathered = feat_table[clamped].astype(jnp.float32)]
    cos x48 -> x0, other arithmetic: 49.8 us -> none  [phase_tile(): return (chosen, jnp.concatenate([jnp.cos(angle), jnp.sin(angle)], axis=0))]
    dot_general x55 -> x0, matrix products: 34.4 us -> none  [the longest x24 13.1 us: accumulate(): lax.dot_general(charges, tile, (((1,), (1,)), ((), ())), precision=highes...]
    pallas_call x0 -> x3, Pallas kernels: none -> 20.8 us  [the longest x1 13.4 us: per_device(): pl.pallas_call(functools.partial(ewald_kernel, sizes, cells, atoms * coun...]
    ppermute x12 -> x0, starting transfers between devices: 19.2 us -> none  [from_behind(): return lax.ppermute(value, axis, pairs)]
    all_to_all x0 -> x1, blocking collectives: none -> 11.6 us  [per_device(): sums = lax.all_to_all(outgoing, axes, 0, 0, tiled=True)]
    reduce_sum x30 -> x0, other arithmetic: 9.39 us -> none  [the longest x2 7.31 us: message_block(): jnp.sum(jnp.where(live_mask, edge_weight * gathered, 0.0), axis=0)]
  transfers between devices with their start and end apart: 13 -> 1, of which waited for: 3 -> 1; matrix products, arithmetic and copies ran while one was open for 15% -> 1% of each run, Pallas kernels for 0% -> 0%
where the time goes in v1:
time: 50.7 us; the launch traced here: 50.4 us
  Pallas kernels  20.8 us (41%)
  blocking collectives  11.6 us (23%)
  waiting for transfers between devices  8.56 us (17%)
  starting transfers between devices  7.33 us (14%)
  local copies, waits for them, and re-layouts  1.41 us (3%)
  between operations  0.65 us (1%)
    pallas_call x1, Pallas kernels, per_device(): pl.pallas_call(functools.partial(ewald_kernel, sizes, cells, atoms * coun...  13.4 us
    all_to_all x1, blocking collectives, per_device(): sums = lax.all_to_all(outgoing, axes, 0, 0, tiled=True)  11.6 us
    all_to_all x1, waiting for transfers between devices, per_device(): received = lax.all_to_all(outgoing, axes, 0, 0, tiled=True)  8.56 us
    all_to_all x1, starting transfers between devices, per_device(): received = lax.all_to_all(outgoing, axes, 0, 0, tiled=True)  7.33 us
    pallas_call x1, Pallas kernels, per_device(): pl.pallas_call(functools.partial(charge_kernel, sizes, cells), out_shape=...  5.67 us
    pallas_call x1, Pallas kernels, per_device(): pl.pallas_call(functools.partial(pack_kernel, sizes), out_shape=jax.Shape...  1.7 us
    unnamed x5, local copies, waits for them, and re-layouts  1.41 us
  transfers between devices with their start and end apart: 1, of which 1 were waited for; matrix products, arithmetic and copies ran while one was open for 1% of the time, Pallas kernels for 0%

profile of v1, /device:TPU:0, one launch (start us, length us, event | category | flops | bytes accessed | tf_op | source)
XLA Modules:
  0.0 50.4 jit_solution(3343245314800059037)
XLA Ops:
  0.6 1.7 %shard_map.122 = bf16[32,24,128]{2,1,0:T(8,128)(2,1)} custom-call(bf16[3,128]{1,0:T(4,128)(2,1)} %pos_ref.3, s32[1,128]{1,0:T(1,128)} %bitcast.1, s32[64,128]{1,0:T(8,128)} %nbr_ref.3, s32[4,32]{1,0:T(4,128)} %rows_ref.1), custom_call_target="tpu_custom_call" | custom-call | tf_op jit(solution)/shard_map/pallas_call | solution.py:498
  2.3 0.0 copy-start.1
  2.3 7.3 %all-to-all-start = ((bf16[32,24,128]{2,1,0:T(8,128)(2,1)}), bf16[32,24,128]{2,1,0:T(8,128)(2,1)S(1)}, u32[]{:S(2)}, u32[]{:S(2)}) async-start(bf16[32,24,128]{2,1,0:T(8,128)(2,1)} %shard_map.122), calls=%async_computation | async-start | bytes 393216 | tf_op jit(solution)/shard_map/all_to_all | solution.py:504
  9.7 0.0 copy-done.1
  9.7 0.7 %copy.13.w_charge_ref = bf16[128,8]{1,0:T(8,128)(2,1)} copy(bf16[128,8]{0,1:T(8,128)(2,1)S(1)} %copy-done.1) | data formatting | bytes 4096 | tf_op args[10]
  10.4 8.6 %all-to-all-done.recv_ref = bf16[32,24,128]{2,1,0:T(8,128)(2,1)S(1)} async-done(((bf16[32,24,128]{2,1,0:T(8,128)(2,1)}), bf16[32,24,128]{2,1,0:T(8,128)(2,1)S(1)}, u32[]{:S(2)}, u32[]{:S(2)}) %all-to-all-start) | async-done | bytes 196640 | tf_op jit(solution)/shard_map/all_to_all | solution.py:504
  19.0 0.0 copy-start
  19.0 0.7 %copy-done = bf16[32,24,128]{2,1,0:T(8,128)(2,1)} copy-done((bf16[32,24,128]{2,1,0:T(8,128)(2,1)}, bf16[32,24,128]{2,1,0:T(8,128)(2,1)S(1)}, u32[]{:S(2)}) %copy-start) | copy-done | bytes 196632
  19.6 5.7 %shard_map.123 = (bf16[32,16,128]{2,1,0:T(8,128)(2,1)}, f32[8,128]{1,0:T(8,128)}) custom-call(bf16[32,24,128]{2,1,0:T(8,128)(2,1)} %copy-done, s32[64,128]{1,0:T(8,128)} %nbr_ref.3, s32[3,12288]{1,0:T(4,128)} %wave_ref.1, bf16[2,128]{1,0:T(2,128)(2,1)} %emb_ref.1, bf16[2,128,128]{2,1,0:T(8,128)(2,1)} %w_in_ref.1, bf16[2,8,128]{2,1,0:T(8,128)(2,1)} %radial_ref.1, ...), custom_call_target="tpu_custom_call" | custom-call | tf_op jit(solution)/shard_map/pallas_call | solution.py:507
  25.3 11.6 %all_to_all.10.sum_ref = bf16[32,16,128]{2,1,0:T(8,128)(2,1)} all-to-all(bf16[32,16,128]{2,1,0:T(8,128)(2,1)} %get-tuple-element.4), channel_id=1, replica_groups=mesh['dom'=8,'sub'=4] {'dom','sub'}, dimensions={0} | all-to-all | bytes 262144 | tf_op jit(solution)/shard_map/all_to_all | solution.py:516
  37.0 13.4 %shard_map.124 = (f32[8,128]{1,0:T(8,128)}, f32[3,128]{1,0:T(4,128)}) custom-call(bf16[32,24,128]{2,1,0:T(8,128)(2,1)} %copy-done, bf16[32,16,128]{2,1,0:T(8,128)(2,1)} %all_to_all.10.sum_ref, f32[8,128]{1,0:T(8,128)} %get-tuple-element.5.charge_ref, bf16[3,128]{1,0:T(4,128)(2,1)} %pos_ref.3), custom_call_target="tpu_custom_call" | custom-call | tf_op jit(solution)/shard_map/pallas_call | solution.py:519
Async XLA Ops:
  2.3 7.3 %copy-start.1 = (bf16[128,8]{0,1:T(8,128)(2,1)S(1)}, bf16[128,8]{0,1:T(8,128)(2,1)}, u32[]{:S(2)}) copy-start(bf16[128,8]{0,1:T(8,128)(2,1)} %param.21) | copy-start | bytes 6148
  2.3 16.6 %all-to-all-start = ((bf16[32,24,128]{2,1,0:T(8,128)(2,1)}), bf16[32,24,128]{2,1,0:T(8,128)(2,1)S(1)}, u32[]{:S(2)}, u32[]{:S(2)}) async-start(bf16[32,24,128]{2,1,0:T(8,128)(2,1)} %shard_map.122), calls=%async_computation | async-start | bytes 393216 | tf_op jit(solution)/shard_map/all_to_all | solution.py:504
  19.0 0.7 %copy-start = (bf16[32,24,128]{2,1,0:T(8,128)(2,1)}, bf16[32,24,128]{2,1,0:T(8,128)(2,1)S(1)}, u32[]{:S(2)}) copy-start(bf16[32,24,128]{2,1,0:T(8,128)(2,1)S(1)} %all-to-all-done.recv_ref) | copy-start | bytes 589828

commit v2 on v1

--- a/solution.py
+++ b/solution.py
@@ -168,18 +168,58 @@
     return (normed / (1.0 + jnp.exp(-normed))).astype(bf16)
 
 
+def ready_kernel(sizes, cells, nbr_ref, wave_ref, emb_ref, w_in_ref, radial_ref, gain_ref, w_out_ref, w_charge_ref, times_ref, column_ref, weight_ref, turned_ref, mask_ref, list_ref):
+    atoms = nbr_ref.shape[1]
+    slots = nbr_ref.shape[0]
+    bases = radial_ref.shape[1]
+    channels = w_in_ref.shape[1]
+    latent = w_charge_ref.shape[0]
+
+    kinds = jnp.concatenate([emb_ref[...].astype(f32), jnp.zeros((6, channels), f32)], axis=0).astype(bf16)
+    two_feats = dot(kinds, w_in_ref[0], ((1,), (0,))).astype(bf16).astype(f32)
+    radial_first = radial_ref[0].astype(f32)
+    weights = jnp.concatenate(
+        [
+            jnp.broadcast_to(radial_first[basis : basis + 1] * two_feats[kind : kind + 1], (8, channels))
+            for kind in range(2)
+            for basis in range(bases)
+        ],
+        axis=0,
+    )
+    weight_ref[...] = weights.T
+    params = jnp.concatenate(
+        [radial_ref[1].astype(f32), gain_ref[...].astype(f32), jnp.zeros((16 - bases - 2, channels), f32)], axis=0
+    ).astype(bf16)
+    width = column_ref.shape[1]
+    spread = jnp.where(iota((16, width), 0) == lanes_of((16, width), atoms), 1.0, 0.0).astype(bf16)
+    column_ref[...] = dot(params, spread, ((0,), (0,)))
+    for place, weight in enumerate((w_out_ref[0], w_in_ref[1], w_out_ref[1])):
+        turned_ref[place * channels : (place + 1) * channels, :] = weight.astype(f32).T.astype(bf16)
+    turned_ref[3 * channels : 3 * channels + 16, :] = jnp.concatenate(
+        [w_charge_ref[...].astype(f32), emb_ref[...].astype(f32), jnp.zeros((16 - 2 - latent, channels), f32)], axis=0
+    ).astype(bf16)
+    listed = [nbr_ref[8 * s : 8 * s + 8, :].astype(f32) for s in range(slots // 8)]
+    for half in range(2):
+        row_number = (iota((atoms, atoms), 0) + half * atoms).astype(f32)
+        times = jnp.zeros((atoms, atoms), f32)
+        for slot in range(slots):
+            times = times + jnp.where(row_number == row_of(listed[slot // 8], slot % 8, atoms), 1.0, 0.0)
+        times_ref[half * atoms : (half + 1) * atoms, :] = times
+    device = lax.axis_index("dom") * sizes[1] + lax.axis_index("sub")
+    mask_ref[...] = wave_mask(wave_ref, cells, device)
+    list_ref[...] = nbr_ref[...]
+
+
 def charge_kernel(
     sizes,
     cells,
     recv_ref,
+    times_ref,
+    column_ref,
+    weight_ref,
+    turned_ref,
+    mask_ref,
     nbr_ref,
-    wave_ref,
-    emb_ref,
-    w_in_ref,
-    radial_ref,
-    gain_ref,
-    w_out_ref,
-    w_charge_ref,
     out_ref,
     charge_ref,
 ):
@@ -187,8 +227,9 @@
     count = out_ref.shape[0]
     atoms = nbr_ref.shape[1]
     slots = nbr_ref.shape[0]
-    bases = radial_ref.shape[1]
-    channels = w_in_ref.shape[1]
+    channels = column_ref.shape[0]
+    bases = column_ref.shape[1] // atoms - 2
+    latent = charge_ref.shape[0]
     ghosts = atoms // 4
     quarter = slots // 4
     dom, sub = lax.axis_index("dom"), lax.axis_index("sub")
@@ -232,52 +273,29 @@
         ],
         axis=1,
     )
-    kinds = jnp.concatenate([emb_ref[...].astype(f32), jnp.zeros((6, channels), f32)], axis=0).astype(bf16)
-    two_feats = dot(kinds, w_in_ref[0], ((1,), (0,))).astype(bf16).astype(f32)
-    radial_first = radial_ref[0].astype(f32)
-    weights = jnp.concatenate(
-        [
-            jnp.broadcast_to(radial_first[basis : basis + 1] * two_feats[kind : kind + 1], (8, channels))
-            for kind in range(2)
-            for basis in range(bases)
-        ],
-        axis=0,
-    )
-    message = dot(weights, sums, ((0,), (0,)), highest)
-
-    params = jnp.concatenate(
-        [radial_ref[1].astype(f32), gain_ref[...].astype(f32), jnp.zeros((16 - bases - 2, channels), f32)], axis=0
-    ).astype(bf16)
-    spread = jnp.where(iota((16, 16 * atoms), 0) == lanes_of((16, 16 * atoms), atoms), 1.0, 0.0).astype(bf16)
-    columns = dot(params, spread, ((0,), (0,)))
+    message = dot(weight_ref[...], sums, ((1,), (0,)), highest)
 
     def column(number):
-        return columns[:, number * atoms : (number + 1) * atoms]
+        return column_ref[:, number * atoms : (number + 1) * atoms]
+
+    def turned(place):
+        return turned_ref[place * channels : (place + 1) * channels, :]
 
     gain_first = column(bases)
     activated = normed_silu(message, jnp.concatenate([gain_first, gain_first], axis=1))
     species = jnp.concatenate([own[3:4], own_ghosts[3:4]], axis=1)
-    kind_rows = iota((8, 2 * atoms), 0)
-    choice = jnp.where((kind_rows < 2) & (jnp.where(species > 0.5, 1, 0) == kind_rows), 1.0, 0.0).astype(bf16)
-    hidden = dot(kinds, choice, ((0,), (0,)))
-    hidden = (hidden + dot(w_out_ref[0], activated, ((0,), (0,)))).astype(bf16)
-    feats = dot(w_in_ref[1], hidden, ((0,), (0,))).astype(bf16)
-
-    near = [cos_sin(jnp.concatenate([own, own_ghosts], axis=1))]
+    kind_rows = iota((16, 2 * atoms), 0) - latent
+    choice = jnp.where(jnp.where(species > 0.5, 1, 0) == kind_rows, 1.0, 0.0).astype(bf16)
+    last = turned_ref[3 * channels : 3 * channels + 16, :]
+    hidden = dot(last, choice, ((0,), (0,)))
+    hidden = (hidden + dot(turned(0), activated, ((1,), (0,)))).astype(bf16)
+    feats = dot(turned(1), hidden, ((1,), (0,))).astype(bf16)
+
+    cosines, sines = cos_sin(jnp.concatenate([own, own_ghosts], axis=1))
     is_axis = iota((8, 2 * atoms), 0) < 3
-    cosines = jnp.where(is_axis, near[0][0], 0.0)
-    sines = jnp.where(is_axis, near[0][1], 0.0)
-    waves = jnp.concatenate([cosines, sines], axis=0)
+    waves = jnp.concatenate([jnp.where(is_axis, cosines, 0.0), jnp.where(is_axis, sines, 0.0)], axis=0)
     chord = 1.5 - 0.5 * dot(waves, waves[:, :atoms], ((0,), (0,)), highest)
-    listed = [nbr_ref[8 * s : 8 * s + 8, :].astype(f32) for s in range(slots // 8)]
-    halves = []
-    for half in range(2):
-        row_number = (iota((atoms, atoms), 0) + half * atoms).astype(f32)
-        times = jnp.zeros((atoms, atoms), f32)
-        for slot in range(slots):
-            times = times + jnp.where(row_number == row_of(listed[slot // 8], slot % 8, atoms), 1.0, 0.0)
-        halves.append(times)
-    times = jnp.concatenate(halves, axis=0)
+    times = times_ref[...]
     power = jnp.exp(-0.125 * chord)
     message = jnp.zeros((channels, atoms), f32)
     for basis in range(bases):
@@ -289,12 +307,11 @@
         mixed = dot(feats, high, ((1,), (0,))) + dot(feats, low, ((1,), (0,)))
         message = message + column(basis) * mixed
     activated = normed_silu(message, column(bases + 1))
-    hidden = (hidden[:, :atoms].astype(f32) + dot(w_out_ref[1], activated, ((0,), (0,)))).astype(bf16)
-    charges = dot(w_charge_ref[...], hidden, ((0,), (0,)))
+    hidden = (hidden[:, :atoms].astype(f32) + dot(turned(2), activated, ((1,), (0,)))).astype(bf16)
+    charges = dot(last, hidden, ((1,), (0,)))[:latent]
     charge_ref[...] = charges
-    mask = wave_mask(wave_ref, cells, dom * n_sub + sub)
-    fill = out_ref.shape[1] - charges.shape[0] - cells
-    pieces = [charges, mask] + ([jnp.zeros((fill, atoms), f32)] if fill else [])
+    fill = out_ref.shape[1] - latent - cells
+    pieces = [charges, mask_ref[...]] + ([jnp.zeros((fill, atoms), f32)] if fill else [])
     block = jnp.concatenate(pieces, axis=0).astype(bf16)
     for device in range(count):
         out_ref[device] = block
@@ -351,54 +368,163 @@
     return first, second
 
 
-def ewald_kernel(sizes, cells, total_atoms, recv_ref, sum_ref, charge_ref, pos_ref, pot_ref, force_ref, grid_ref, left_ref, prod_ref, mask_ref, mix_ref):
-    n_dom, n_sub = sizes
-    latent, atoms = charge_ref.shape
-    count = recv_ref.shape[0]
-    chunk = grid_ref.shape[1] // atoms
-    rows = latent * 2 * harmonics
-
-    def build(device, place):
-        coords = recv_ref[device, 0:common, :].astype(f32)
-        tables = harmonic_tables(coords)
+def fill_grid(recv_ref, device, place, grid_ref, third_ref, skipped=0):
+    atoms = recv_ref.shape[2]
+    tables = harmonic_tables(recv_ref[device, 0:common, :].astype(f32))
+    spot = pl.ds(pl.multiple_of(place * atoms, atoms), atoms)
+    third_spot = pl.ds(pl.multiple_of((place + skipped) * atoms, atoms), atoms)
+    for kind in range(2):
+        for piece in range(3):
+            third_ref[24 * kind + 8 * piece : 24 * kind + 8 * piece + 8, third_spot] = tables[2][kind][piece]
+    for kind in range(4):
+        groups = pair_rows(tables[0][kind // 2], tables[1][kind % 2])
+        for at in range(0, pair_groups, 2):
+            start = kind * pairs + at * 8
+            grid_ref[start : start + 16, spot] = jnp.concatenate(groups[at : at + 2], axis=0).astype(bf16)
+
+
+def own_tables(recv_ref, sizes):
+    device = lax.axis_index("dom") * sizes[1] + lax.axis_index("sub")
+    return harmonic_tables(recv_ref[device, 0:common, :].astype(f32))
+
+
+def own_side(recv_ref, sizes, right_ref):
+    atoms = recv_ref.shape[2]
+    tables = own_tables(recv_ref, sizes)
+    first, second = pair_values(iota((pairs, atoms), 0))
+    first, second = first.astype(f32), second.astype(f32)
+    basis = [jnp.concatenate(pair_rows(tables[0][kind // 2], tables[1][kind % 2]), axis=0) for kind in range(4)]
+    along_x = [-first * basis[2], -first * basis[3], first * basis[0], first * basis[1]]
+    along_y = [-second * basis[1], second * basis[0], -second * basis[3], second * basis[2]]
+    for d, part in enumerate((basis, along_x, along_y)):
+        for kind in range(4):
+            right_ref[kind * pairs : (kind + 1) * pairs, d * atoms : (d + 1) * atoms] = part[kind].astype(bf16)
+
+
+def grid_kernel(sizes, recv_ref, out_ref, third_ref, right_ref, grid_ref, sems):
+    chunks, _, width = out_ref.shape
+    atoms = recv_ref.shape[2]
+    blocks = width // atoms
+    copies = [pltpu.make_async_copy(grid_ref.at[c], out_ref.at[c], sems.at[c]) for c in range(chunks)]
+    for c in range(chunks):
+
+        def one(place, carry):
+            fill_grid(recv_ref, c * blocks + place, place, grid_ref.at[c], third_ref, c * blocks)
+            return carry
+
+        lax.fori_loop(0, blocks, one, 0)
+        copies[c].start()
+    own_side(recv_ref, sizes, right_ref)
+    for copy in copies:
+        copy.wait()
+
+
+def make_left(sum_ref, third_ref, left_ref, latent, first_device, chunk):
+    atoms = sum_ref.shape[2]
+
+    def one(place, inner):
         spot = pl.ds(pl.multiple_of(place * atoms, atoms), atoms)
-        charge = sum_ref[device, 0:latent, :].astype(f32)
+        charge = sum_ref[first_device + place, 0:latent, :].astype(f32)
         left = []
         for kind in range(2):
-            left += [charge * row_of(tables[2][kind][m // 8], m % 8, latent) for m in range(harmonics)]
+            for m in range(harmonics):
+                left.append(charge * jnp.broadcast_to(third_ref[24 * kind + m : 24 * kind + m + 1, spot], (latent, atoms)))
         for at in range(0, 2 * harmonics, 2):
             left_ref[at * latent : (at + 2) * latent, spot] = jnp.concatenate(left[at : at + 2], axis=0).astype(bf16)
-        for kind in range(4):
-            groups = pair_rows(tables[0][kind // 2], tables[1][kind % 2])
-            for at in range(0, pair_groups, 2):
-                start = kind * pairs + at * 8
-                grid_ref[start : start + 16, spot] = jnp.concatenate(groups[at : at + 2], axis=0).astype(bf16)
+        return inner
+
+    lax.fori_loop(0, chunk, one, 0)
+
+
+def tiled_ewald_kernel(
+    cells,
+    total_atoms,
+    sizes,
+    sum_ref,
+    charge_ref,
+    recv_ref,
+    third_ref,
+    right_ref,
+    grid_ref,
+    pot_ref,
+    force_ref,
+    left_ref,
+    prod_ref,
+    mask_ref,
+    mix_ref,
+    held_ref,
+    sems,
+):
+    chunks, total, width = grid_ref.shape
+    tiles, start = [], 0
+    for size in (256, 256, 512, 512):
+        tiles.append((start, size))
+        start += size
+    copies = [
+        [
+            pltpu.make_async_copy(
+                grid_ref.at[c, start : start + size, :],
+                held_ref.at[start : start + size, c * width : (c + 1) * width],
+                sems.at[number, c],
+            )
+            for c in range(chunks)
+        ]
+        for number, (start, size) in enumerate(tiles)
+    ]
+    for group in copies:
+        for copy in group:
+            copy.start()
+    make_left(sum_ref, third_ref, left_ref, charge_ref.shape[0], 0, sum_ref.shape[0])
+    for group, (start, size) in zip(copies, tiles, strict=True):
+        for copy in group:
+            copy.wait()
+        prod_ref[:, start : start + size] = dot(left_ref[...], held_ref[start : start + size, :], ((1,), (1,)))
+    apply_sums(cells, total_atoms, sizes, sum_ref, charge_ref, recv_ref, right_ref, pot_ref, force_ref, prod_ref, mask_ref, mix_ref)
+
+
+def chunked_ewald_kernel(
+    cells,
+    total_atoms,
+    sizes,
+    sum_ref,
+    charge_ref,
+    recv_ref,
+    pot_ref,
+    force_ref,
+    left_ref,
+    prod_ref,
+    mask_ref,
+    mix_ref,
+    grid_ref,
+    third_ref,
+    right_ref,
+):
+    atoms = charge_ref.shape[1]
+    chunk = grid_ref.shape[1] // atoms
+    own_side(recv_ref, sizes, right_ref)
+    prod_ref[...] = jnp.zeros(prod_ref.shape, f32)
 
     def whole_chunk(number, carry):
         def one(place, inner):
-            build(number * chunk + place, place)
+            fill_grid(recv_ref, number * chunk + place, place, grid_ref, third_ref)
             return inner
 
         lax.fori_loop(0, chunk, one, 0)
+        make_left(sum_ref, third_ref, left_ref, charge_ref.shape[0], number * chunk, chunk)
 
         def tile(column, inner):
             spot = pl.ds(pl.multiple_of(column * 256, 256), 256)
-            part = dot(left_ref[...], grid_ref[spot, :], ((1,), (1,)))
-
-            @pl.when(number == 0)
-            def _():
-                prod_ref[:, spot] = part
-
-            @pl.when(number > 0)
-            def _():
-                prod_ref[:, spot] = prod_ref[:, spot] + part
-
+            prod_ref[:, spot] = prod_ref[:, spot] + dot(left_ref[...], grid_ref[spot, :], ((1,), (1,)))
             return inner
 
         return lax.fori_loop(0, 4 * pairs // 256, tile, carry)
 
-    lax.fori_loop(0, count // chunk, whole_chunk, 0)
-
+    lax.fori_loop(0, sum_ref.shape[0] // chunk, whole_chunk, 0)
+    apply_sums(cells, total_atoms, sizes, sum_ref, charge_ref, recv_ref, right_ref, pot_ref, force_ref, prod_ref, mask_ref, mix_ref)
+
+
+def apply_sums(cells, total_atoms, sizes, sum_ref, charge_ref, recv_ref, right_ref, pot_ref, force_ref, prod_ref, mask_ref, mix_ref):
+    latent, atoms = charge_ref.shape
     for device in range(-(-mask_rows // cells)):
         mask_ref[device * cells : (device + 1) * cells, :] = sum_ref[device, latent : latent + cells, :].astype(f32)
     first, second = pair_values(iota((8, pairs), 1))
@@ -442,17 +568,8 @@
                             mixed = mixed + term if signs[i] == signs[j] else mixed - term
                     mix_ref[place] = mixed
 
-    coords = jnp.concatenate([pos_ref[...].astype(f32), jnp.zeros((5, atoms), f32)], axis=0)
-    tables = harmonic_tables(coords)
-    first, second = pair_values(iota((pairs, atoms), 0))
-    first, second = first.astype(f32), second.astype(f32)
-    basis = [jnp.concatenate(pair_rows(tables[0][kind // 2], tables[1][kind % 2]), axis=0) for kind in range(4)]
-    along_x = [-first * basis[2], -first * basis[3], first * basis[0], first * basis[1]]
-    along_y = [-second * basis[1], second * basis[0], -second * basis[3], second * basis[2]]
-    right = jnp.concatenate(
-        [jnp.concatenate(part, axis=0).astype(bf16) for part in (basis, along_x, along_y)], axis=1
-    )
-    product = dot(mix_ref[...].astype(bf16), right, ((1,), (0,)))
+    tables = own_tables(recv_ref, sizes)
+    product = dot(mix_ref[...].astype(bf16), right_ref[...], ((1,), (0,)))
     potential = jnp.zeros((latent, atoms), f32)
     slopes = [jnp.zeros((latent, atoms), f32) for _ in range(3)]
     for u in range(2):
@@ -495,6 +612,7 @@
     atoms = positions.shape[1]
     latent = w_charge.shape[1]
     slots = neighbours.shape[0]
+    params = pltpu.CompilerParams(vmem_limit_bytes=32 * 1024 * 1024)
     outgoing = pl.pallas_call(
         functools.partial(pack_kernel, sizes),
         out_shape=jax.ShapeDtypeStruct((count, common + slots // 4, atoms), bf16),
@@ -503,6 +621,22 @@
     )(positions, species[None, :], neighbours, ghost_rows)
     received = lax.all_to_all(outgoing, axes, 0, 0, tiled=True)
     cells = -(-mask_rows // count)
+    channels = w_in.shape[1]
+    bases = radial.shape[1]
+    ready = pl.pallas_call(
+        functools.partial(ready_kernel, sizes, cells),
+        out_shape=(
+            jax.ShapeDtypeStruct((2 * atoms, atoms), f32),
+            jax.ShapeDtypeStruct((channels, (bases + 2) * atoms), f32),
+            jax.ShapeDtypeStruct((channels, 16 * bases), f32),
+            jax.ShapeDtypeStruct((3 * channels + 16, channels), bf16),
+            jax.ShapeDtypeStruct((cells, atoms), f32),
+            jax.ShapeDtypeStruct((slots, atoms), i32),
+        ),
+        in_specs=vmem(8),
+        out_specs=tuple(vmem(6)),
+        compiler_params=params,
+    )(neighbours, wavevectors, embedding, w_in, radial, norm_gain, w_out, w_charge.T)
     rows_out = -(-(latent + cells) // 8) * 8
     outgoing, charges = pl.pallas_call(
         functools.partial(charge_kernel, sizes, cells),
@@ -510,28 +644,61 @@
             jax.ShapeDtypeStruct((count, rows_out, atoms), bf16),
             jax.ShapeDtypeStruct((latent, atoms), f32),
         ),
-        in_specs=vmem(9),
+        in_specs=vmem(7),
         out_specs=tuple(vmem(2)),
-    )(received, neighbours, wavevectors, embedding, w_in, radial, norm_gain, w_out, w_charge)
+        compiler_params=params,
+    )(received, *ready)
     sums = lax.all_to_all(outgoing, axes, 0, 0, tiled=True)
     chunk = math.gcd(count, 32)
     rows = latent * 2 * harmonics
+    results = (
+        jax.ShapeDtypeStruct((latent, atoms), f32),
+        jax.ShapeDtypeStruct((3, atoms), f32),
+    )
+    tables = (
+        ((4 * pairs, chunk * atoms), bf16),
+        ((48, chunk * atoms), f32),
+        ((4 * pairs, 3 * atoms), bf16),
+    )
+    scratch = [
+        pltpu.VMEM((rows, chunk * atoms), bf16),
+        pltpu.VMEM((rows, 4 * pairs), f32),
+        pltpu.VMEM((-(-mask_rows // cells) * cells, 128), f32),
+        pltpu.VMEM((rows, 4 * pairs), f32),
+    ]
+    if chunk < count:
+        return pl.pallas_call(
+            functools.partial(chunked_ewald_kernel, cells, atoms * count, sizes),
+            out_shape=results,
+            in_specs=vmem(3),
+            out_specs=tuple(vmem(2)),
+            scratch_shapes=scratch + [pltpu.VMEM(*table) for table in tables],
+        )(sums, charges, received)
+    chunks = count // math.gcd(count, 4)
+    hbm = pl.BlockSpec(memory_space=pltpu.HBM)
+    grid, third, right = pl.pallas_call(
+        functools.partial(grid_kernel, sizes),
+        out_shape=(
+            pltpu.HBM((chunks, 4 * pairs, count * atoms // chunks), bf16),
+            jax.ShapeDtypeStruct(*tables[1]),
+            jax.ShapeDtypeStruct(*tables[2]),
+        ),
+        in_specs=vmem(1),
+        out_specs=(hbm, *vmem(2)),
+        scratch_shapes=[
+            pltpu.VMEM((chunks, 4 * pairs, count * atoms // chunks), bf16),
+            pltpu.SemaphoreType.DMA((chunks,)),
+        ],
+        compiler_params=params,
+    )(received)
     return pl.pallas_call(
-        functools.partial(ewald_kernel, sizes, cells, atoms * count),
-        out_shape=(
-            jax.ShapeDtypeStruct((latent, atoms), f32),
-            jax.ShapeDtypeStruct((3, atoms), f32),
-        ),
-        in_specs=vmem(4),
+        functools.partial(tiled_ewald_kernel, cells, atoms * count, sizes),
+        out_shape=results,
+        in_specs=vmem(5) + [hbm],
         out_specs=tuple(vmem(2)),
-        scratch_shapes=[
-            pltpu.VMEM((4 * pairs, chunk * atoms), bf16),
-            pltpu.VMEM((rows, chunk * atoms), bf16),
-            pltpu.VMEM((rows, 4 * pairs), f32),
-            pltpu.VMEM((-(-mask_rows // cells) * cells, 128), f32),
-            pltpu.VMEM((rows, 4 * pairs), f32),
-        ],
-    )(received, sums, charges, positions)
+        scratch_shapes=scratch + [pltpu.VMEM(*tables[0]), pltpu.SemaphoreType.DMA((4, chunks))],
+        compiler_params=params,
+    )(sums, charges, received, third, right, pltpu.with_memory_space_constraint(grid, pltpu.HBM))
 
 
 def solution(mesh):

time: 50.7 us -> 45.1 us (0.89)
  blocking collectives: 11.6 us -> 0 us
  local copies, waits for them, and re-layouts: 1.41 us -> 6.03 us
  starting transfers between devices: 7.33 us -> 11.3 us
  waiting for transfers between devices: 8.56 us -> 5.26 us
    all_to_all x1 -> x0, blocking collectives: 11.6 us -> none  [per_device(): sums = lax.all_to_all(outgoing, axes, 0, 0, tiled=True)]
    all_to_all x1, waiting for transfers between devices: 8.56 us -> 1.88 us  [per_device(): received = lax.all_to_all(outgoing, axes, 0, 0, tiled=True)]
    unnamed x5 -> x16, local copies, waits for them, and re-layouts: 1.41 us -> 6.03 us
    all_to_all x0 -> x1, starting transfers between devices: none -> 3.99 us  [per_device(): sums = lax.all_to_all(outgoing, axes, 0, 0, tiled=True)]
    all_to_all x0 -> x1, waiting for transfers between devices: none -> 3.39 us  [per_device(): sums = lax.all_to_all(outgoing, axes, 0, 0, tiled=True)]
    pallas_call x1 -> x3, Pallas kernels: 13.4 us -> 16.3 us  [the longest x1 9.93 us: per_device(): pl.pallas_call(functools.partial(tiled_ewald_kernel, cells, atoms * count...]
    pallas_call x1, Pallas kernels: 5.67 us -> 3.21 us  [per_device(): pl.pallas_call(functools.partial(charge_kernel, sizes, cells), out_shape=...]
  transfers between devices with their start and end apart: 1 -> 2, of which waited for: 1 -> 2; matrix products, arithmetic and copies ran while one was open for 1% -> 0% of each run, Pallas kernels for 0% -> 14%
where the time goes in v2:
time: 45.1 us; the launch traced here: 44.5 us
  Pallas kernels  21.2 us (47%)
  starting transfers between devices  11.3 us (25%)
  local copies, waits for them, and re-layouts  6.03 us (13%)
  waiting for transfers between devices  5.26 us (12%)
  between operations  0.68 us (2%)
    pallas_call x1, Pallas kernels, per_device(): pl.pallas_call(functools.partial(tiled_ewald_kernel, cells, atoms * count...  9.93 us
    all_to_all x1, starting transfers between devices, per_device(): received = lax.all_to_all(outgoing, axes, 0, 0, tiled=True)  7.33 us
    unnamed x16, local copies, waits for them, and re-layouts  6.03 us
    pallas_call x1, Pallas kernels, per_device(): pl.pallas_call(functools.partial(grid_kernel, sizes), out_shape=(pltpu.HB...  4.98 us
    all_to_all x1, starting transfers between devices, per_device(): sums = lax.all_to_all(outgoing, axes, 0, 0, tiled=True)  3.99 us
    all_to_all x1, waiting for transfers between devices, per_device(): sums = lax.all_to_all(outgoing, axes, 0, 0, tiled=True)  3.39 us
    pallas_call x1, Pallas kernels, per_device(): pl.pallas_call(functools.partial(charge_kernel, sizes, cells), out_shape=...  3.21 us
    all_to_all x1, waiting for transfers between devices, per_device(): received = lax.all_to_all(outgoing, axes, 0, 0, tiled=True)  1.88 us
  transfers between devices with their start and end apart: 2, of which 2 were waited for; matrix products, arithmetic and copies ran while one was open for 0% of the time, Pallas kernels for 14%

profile of v2, /device:TPU:0, one launch (start us, length us, event | category | flops | bytes accessed | tf_op | source)
XLA Modules:
  0.0 44.5 jit_solution(10729612098044775839)
XLA Ops:
  0.6 1.7 %shard_map.122 = bf16[32,24,128]{2,1,0:T(8,128)(2,1)} custom-call(bf16[3,128]{1,0:T(4,128)(2,1)} %pos_ref.1, s32[1,128]{1,0:T(1,128)} %bitcast.3, s32[64,128]{1,0:T(8,128)} %nbr_ref.3, s32[4,32]{1,0:T(4,128)} %rows_ref.1), custom_call_target="tpu_custom_call" | custom-call | tf_op jit(solution)/shard_map/pallas_call | solution.py:616
  2.3 7.3 %all-to-all-start = ((bf16[32,24,128]{2,1,0:T(8,128)(2,1)}), bf16[32,24,128]{2,1,0:T(8,128)(2,1)S(1)}, u32[]{:S(2)}, u32[]{:S(2)}) async-start(bf16[32,24,128]{2,1,0:T(8,128)(2,1)} %shard_map.122), calls=%async_computation | async-start | bytes 393216 | tf_op jit(solution)/shard_map/all_to_all | solution.py:622
  9.7 0.0 copy-start
  9.7 0.9 %copy-done = s32[3,12288]{1,0:T(4,128)S(1)} copy-done((s32[3,12288]{1,0:T(4,128)S(1)}, s32[3,12288]{1,0:T(4,128)}, u32[]{:S(2)}) %copy-start) | copy-done | bytes 147480
  10.6 0.0 copy-start.1
  10.6 0.8 %copy-done.1 = s32[64,128]{1,0:T(8,128)S(1)} copy-done((s32[64,128]{1,0:T(8,128)S(1)}, s32[64,128]{1,0:T(8,128)}, u32[]{:S(2)}) %copy-start.1) | copy-done | bytes 32792
  11.4 0.0 copy-start.2
  11.4 0.8 %copy-done.2 = bf16[2,128,128]{2,1,0:T(8,128)(2,1)S(1)} copy-done((bf16[2,128,128]{2,1,0:T(8,128)(2,1)S(1)}, bf16[2,128,128]{2,1,0:T(8,128)(2,1)}, u32[]{:S(2)}) %copy-start.2) | copy-done | bytes 65560
  12.2 0.0 copy-start.3
  12.2 0.8 %copy-done.3 = bf16[2,128,128]{2,1,0:T(8,128)(2,1)S(1)} copy-done((bf16[2,128,128]{2,1,0:T(8,128)(2,1)S(1)}, bf16[2,128,128]{2,1,0:T(8,128)(2,1)}, u32[]{:S(2)}) %copy-start.3) | copy-done | bytes 65560
  13.0 0.0 copy-start.4
  13.0 0.7 %copy-done.4 = bf16[2,8,128]{2,1,0:T(8,128)(2,1)S(1)} copy-done((bf16[2,8,128]{2,1,0:T(8,128)(2,1)S(1)}, bf16[2,8,128]{2,1,0:T(8,128)(2,1)}, u32[]{:S(2)}) %copy-start.4) | copy-done | bytes 4120
  13.7 0.0 copy-start.5
  13.7 0.7 %copy-done.5 = bf16[128,8]{0,1:T(8,128)(2,1)S(1)} copy-done((bf16[128,8]{0,1:T(8,128)(2,1)S(1)}, bf16[128,8]{0,1:T(8,128)(2,1)}, u32[]{:S(2)}) %copy-start.5) | copy-done | bytes 2072
  14.4 0.0 copy-start.6
  14.4 0.7 %copy-done.6 = bf16[2,128]{1,0:T(2,128)(2,1)S(1)} copy-done((bf16[2,128]{1,0:T(2,128)(2,1)S(1)}, bf16[2,128]{1,0:T(2,128)(2,1)}, u32[]{:S(2)}) %copy-start.6) | copy-done | bytes 536
  15.1 0.7 %copy-done.7 = bf16[2,128]{1,0:T(2,128)(2,1)S(1)} copy-done((bf16[2,128]{1,0:T(2,128)(2,1)S(1)}, bf16[2,128]{1,0:T(2,128)(2,1)}, u32[]{:S(2)}) %copy-start.7) | copy-done | bytes 536
  15.7 1.4 %shard_map.123 = (f32[256,128]{1,0:T(8,128)S(1)}, f32[128,1280]{1,0:T(8,128)S(1)}, f32[128,128]{1,0:T(8,128)S(1)}, bf16[400,128]{1,0:T(8,128)(2,1)S(1)}, f32[8,128]{1,0:T(8,128)S(1)}, /*index=5*/s32[64,128]{1,0:T(8,128)S(1)}) custom-call(s32[64,128]{1,0:T(8,128)S(1)} %copy-done.1, s32[3,12288]{1,0:T(4,128)S(1)} %copy-done, bf16[2,128]{1,0:T(2,128)(2,1)S(1)} %copy-done.6, ...), custom_call_target="tpu_custom_call" | custom-call | tf_op jit(solution)/shard_map/pallas_call | solution.py:626
  17.1 1.9 %all-to-all-done.recv_ref = bf16[32,24,128]{2,1,0:T(8,128)(2,1)S(1)} async-done(((bf16[32,24,128]{2,1,0:T(8,128)(2,1)}), bf16[32,24,128]{2,1,0:T(8,128)(2,1)S(1)}, u32[]{:S(2)}, u32[]{:S(2)}) %all-to-all-start) | async-done | bytes 196640 | tf_op jit(solution)/shard_map/all_to_all | solution.py:622
  19.0 3.2 %shard_map.124 = (bf16[32,16,128]{2,1,0:T(8,128)(2,1)}, f32[8,128]{1,0:T(8,128)S(1)}) custom-call(bf16[32,24,128]{2,1,0:T(8,128)(2,1)S(1)} %all-to-all-done.recv_ref, f32[256,128]{1,0:T(8,128)S(1)} %get-tuple-element.13.times_ref, f32[128,1280]{1,0:T(8,128)S(1)} %get-tuple-element.14.column_ref, f32[128,128]{1,0:T(8,128)S(1)} %get-tuple-element.15.weight_ref, ...), custom_call_target="tpu_custom_call" | custom-call | tf_op jit(solution)/shard_map/pallas_call | solution.py:641
  22.2 4.0 %all-to-all-start.1 = ((bf16[32,16,128]{2,1,0:T(8,128)(2,1)}), bf16[32,16,128]{2,1,0:T(8,128)(2,1)S(1)}, u32[]{:S(2)}, u32[]{:S(2)}) async-start(bf16[32,16,128]{2,1,0:T(8,128)(2,1)} %get-tuple-element.19), calls=%async_computation.1 | async-start | bytes 262144 | tf_op jit(solution)/shard_map/all_to_all | solution.py:651
  26.2 5.0 %shard_map.125 = (bf16[8,1536,512]{2,1,0:T(8,128)(2,1)}, f32[48,4096]{1,0:T(8,128)S(1)}, bf16[1536,384]{1,0:T(8,128)(2,1)S(1)}) custom-call(bf16[32,24,128]{2,1,0:T(8,128)(2,1)S(1)} %all-to-all-done.recv_ref), custom_call_target="tpu_custom_call" | custom-call | tf_op jit(solution)/shard_map/pallas_call | solution.py:679
  31.2 3.4 %all-to-all-done.1.sum_ref = bf16[32,16,128]{2,1,0:T(8,128)(2,1)S(1)} async-done(((bf16[32,16,128]{2,1,0:T(8,128)(2,1)}), bf16[32,16,128]{2,1,0:T(8,128)(2,1)S(1)}, u32[]{:S(2)}, u32[]{:S(2)}) %all-to-all-start.1) | async-done | bytes 131104 | tf_op jit(solution)/shard_map/all_to_all | solution.py:651
  34.6 9.9 %shard_map.126 = (f32[8,128]{1,0:T(8,128)}, f32[3,128]{1,0:T(4,128)}) custom-call(bf16[32,16,128]{2,1,0:T(8,128)(2,1)S(1)} %all-to-all-done.1.sum_ref, f32[8,128]{1,0:T(8,128)S(1)} %get-tuple-element.20.charge_ref, bf16[32,24,128]{2,1,0:T(8,128)(2,1)S(1)} %all-to-all-done.recv_ref, f32[48,4096]{1,0:T(8,128)S(1)} %get-tuple-element.21.third_ref, ...), custom_call_target="tpu_custom_call" | custom-call | tf_op jit(solution)/shard_map/pallas_call | solution.py:694
  (1 shorter events, 0.0 us)
Async XLA Ops:
  2.3 16.6 %all-to-all-start = ((bf16[32,24,128]{2,1,0:T(8,128)(2,1)}), bf16[32,24,128]{2,1,0:T(8,128)(2,1)S(1)}, u32[]{:S(2)}, u32[]{:S(2)}) async-start(bf16[32,24,128]{2,1,0:T(8,128)(2,1)} %shard_map.122), calls=%async_computation | async-start | bytes 393216 | tf_op jit(solution)/shard_map/all_to_all | solution.py:622
  9.7 0.9 %copy-start = (s32[3,12288]{1,0:T(4,128)S(1)}, s32[3,12288]{1,0:T(4,128)}, u32[]{:S(2)}) copy-start(s32[3,12288]{1,0:T(4,128)} %wave_ref.1) | copy-start | bytes 442372
  10.6 0.8 %copy-start.1 = (s32[64,128]{1,0:T(8,128)S(1)}, s32[64,128]{1,0:T(8,128)}, u32[]{:S(2)}) copy-start(s32[64,128]{1,0:T(8,128)} %nbr_ref.3) | copy-start | bytes 98308
  11.4 0.8 %copy-start.2 = (bf16[2,128,128]{2,1,0:T(8,128)(2,1)S(1)}, bf16[2,128,128]{2,1,0:T(8,128)(2,1)}, u32[]{:S(2)}) copy-start(bf16[2,128,128]{2,1,0:T(8,128)(2,1)} %w_in_ref.1) | copy-start | bytes 196612
  12.2 0.8 %copy-start.3 = (bf16[2,128,128]{2,1,0:T(8,128)(2,1)S(1)}, bf16[2,128,128]{2,1,0:T(8,128)(2,1)}, u32[]{:S(2)}) copy-start(bf16[2,128,128]{2,1,0:T(8,128)(2,1)} %w_out_ref.1) | copy-start | bytes 196612
  13.0 0.7 %copy-start.4 = (bf16[2,8,128]{2,1,0:T(8,128)(2,1)S(1)}, bf16[2,8,128]{2,1,0:T(8,128)(2,1)}, u32[]{:S(2)}) copy-start(bf16[2,8,128]{2,1,0:T(8,128)(2,1)} %radial_ref.1) | copy-start | bytes 12292
  13.7 0.7 %copy-start.5 = (bf16[128,8]{0,1:T(8,128)(2,1)S(1)}, bf16[128,8]{0,1:T(8,128)(2,1)}, u32[]{:S(2)}) copy-start(bf16[128,8]{0,1:T(8,128)(2,1)} %param.21) | copy-start | bytes 6148
  14.4 0.7 %copy-start.6 = (bf16[2,128]{1,0:T(2,128)(2,1)S(1)}, bf16[2,128]{1,0:T(2,128)(2,1)}, u32[]{:S(2)}) copy-start(bf16[2,128]{1,0:T(2,128)(2,1)} %emb_ref.1) | copy-start | bytes 1540
  15.1 0.7 %copy-start.7 = (bf16[2,128]{1,0:T(2,128)(2,1)S(1)}, bf16[2,128]{1,0:T(2,128)(2,1)}, u32[]{:S(2)}) copy-start(bf16[2,128]{1,0:T(2,128)(2,1)} %gain_ref.1) | copy-start | bytes 1540
  22.2 12.4 %all-to-all-start.1 = ((bf16[32,16,128]{2,1,0:T(8,128)(2,1)}), bf16[32,16,128]{2,1,0:T(8,128)(2,1)S(1)}, u32[]{:S(2)}, u32[]{:S(2)}) async-start(bf16[32,16,128]{2,1,0:T(8,128)(2,1)} %get-tuple-element.19), calls=%async_computation.1 | async-start | bytes 262144 | tf_op jit(solution)/shard_map/all_to_all | solution.py:651

commit v3 on v2

--- a/solution.py
+++ b/solution.py
@@ -138,7 +138,7 @@
     return jnp.concatenate(total[0] + total[1], axis=0)
 
 
-def wave_mask(wave_ref, rows, device):
+def wave_mask(wave_ref):
     first = wave_ref[0:1, :]
     second = wave_ref[1:2, :]
     third = wave_ref[2:3, :]
@@ -149,18 +149,12 @@
         jnp.where(size < 16, 160 + 8 * first + size, jnp.where(size < 20, 304 + 4 * first + size, 376)),
     )
     side = jnp.where(second < 0, 1, 0)
-    block = jnp.right_shift(pair, 7)
+    row = (jnp.right_shift(pair, 7) * 2 + side) * signed + third + (reach - 1)
     lane = jnp.bitwise_and(pair, 127)
-    row = (block * 2 + side) * signed + third + (reach - 1) - device * rows
-    inside = (row >= 0) & (row < rows)
-    key = jnp.where(inside, jnp.right_shift(lane, 5) * rows + row, -1)
-    low = jnp.bitwise_and(lane, 31)
-    total_k = key.shape[1]
-    left = jnp.where(iota((4 * rows, total_k), 0) == key, 1.0, 0.0).astype(bf16)
-    right = jnp.where(iota((32, total_k), 0) == low, 1.0, 0.0).astype(bf16)
-    found = dot(left, right, ((1,), (1,)))
-    spread = jnp.concatenate([found] * 4, axis=1)
-    return by_block([spread[q * rows : (q + 1) * rows] for q in range(4)], 32)
+    total_k = row.shape[1]
+    left = jnp.where(iota((mask_rows, total_k), 0) == row, 1.0, 0.0).astype(bf16)
+    right = jnp.where(iota((128, total_k), 0) == lane, 1.0, 0.0).astype(bf16)
+    return dot(left, right, ((1,), (1,)))
 
 
 def normed_silu(message, gain):
@@ -168,7 +162,7 @@
     return (normed / (1.0 + jnp.exp(-normed))).astype(bf16)
 
 
-def ready_kernel(sizes, cells, nbr_ref, wave_ref, emb_ref, w_in_ref, radial_ref, gain_ref, w_out_ref, w_charge_ref, times_ref, column_ref, weight_ref, turned_ref, mask_ref, list_ref):
+def ready_kernel(nbr_ref, emb_ref, w_in_ref, radial_ref, gain_ref, w_out_ref, w_charge_ref, times_ref, column_ref, weight_ref, turned_ref, list_ref):
     atoms = nbr_ref.shape[1]
     slots = nbr_ref.shape[0]
     bases = radial_ref.shape[1]
@@ -205,20 +199,16 @@
         for slot in range(slots):
             times = times + jnp.where(row_number == row_of(listed[slot // 8], slot % 8, atoms), 1.0, 0.0)
         times_ref[half * atoms : (half + 1) * atoms, :] = times
-    device = lax.axis_index("dom") * sizes[1] + lax.axis_index("sub")
-    mask_ref[...] = wave_mask(wave_ref, cells, device)
     list_ref[...] = nbr_ref[...]
 
 
 def charge_kernel(
     sizes,
-    cells,
     recv_ref,
     times_ref,
     column_ref,
     weight_ref,
     turned_ref,
-    mask_ref,
     nbr_ref,
     out_ref,
     charge_ref,
@@ -310,9 +300,7 @@
     hidden = (hidden[:, :atoms].astype(f32) + dot(turned(2), activated, ((1,), (0,)))).astype(bf16)
     charges = dot(last, hidden, ((1,), (0,)))[:latent]
     charge_ref[...] = charges
-    fill = out_ref.shape[1] - latent - cells
-    pieces = [charges, mask_ref[...]] + ([jnp.zeros((fill, atoms), f32)] if fill else [])
-    block = jnp.concatenate(pieces, axis=0).astype(bf16)
+    block = charges.astype(bf16)
     for device in range(count):
         out_ref[device] = block
 
@@ -368,19 +356,27 @@
     return first, second
 
 
-def fill_grid(recv_ref, device, place, grid_ref, third_ref, skipped=0):
+def fill_products(first, second, kinds, spot, grid_ref):
+    for kind in kinds:
+        groups = pair_rows(first[kind // 2], second[kind % 2])
+        for at in range(0, pair_groups, 2):
+            start = (kind * pair_groups + at) * 8
+            grid_ref[start : start + 16, spot] = jnp.concatenate(groups[at : at + 2], axis=0).astype(bf16)
+
+
+def fill_grid(recv_ref, device, place, grid_ref, third_ref, kinds, skipped=0, flat_ref=None):
     atoms = recv_ref.shape[2]
     tables = harmonic_tables(recv_ref[device, 0:common, :].astype(f32))
     spot = pl.ds(pl.multiple_of(place * atoms, atoms), atoms)
-    third_spot = pl.ds(pl.multiple_of((place + skipped) * atoms, atoms), atoms)
+    later = pl.ds(pl.multiple_of((place + skipped) * atoms, atoms), atoms)
     for kind in range(2):
         for piece in range(3):
-            third_ref[24 * kind + 8 * piece : 24 * kind + 8 * piece + 8, third_spot] = tables[2][kind][piece]
-    for kind in range(4):
-        groups = pair_rows(tables[0][kind // 2], tables[1][kind % 2])
-        for at in range(0, pair_groups, 2):
-            start = kind * pairs + at * 8
-            grid_ref[start : start + 16, spot] = jnp.concatenate(groups[at : at + 2], axis=0).astype(bf16)
+            third_ref[24 * kind + 8 * piece : 24 * kind + 8 * piece + 8, later] = tables[2][kind][piece]
+    if flat_ref is not None:
+        for number, table in enumerate((tables[0][1], tables[1][0], tables[1][1])):
+            for piece in range(3):
+                flat_ref[24 * number + 8 * piece : 24 * number + 8 * piece + 8, later] = table[piece]
+    fill_products(tables[0], tables[1], kinds, spot, grid_ref)
 
 
 def own_tables(recv_ref, sizes):
@@ -401,20 +397,23 @@
             right_ref[kind * pairs : (kind + 1) * pairs, d * atoms : (d + 1) * atoms] = part[kind].astype(bf16)
 
 
-def grid_kernel(sizes, recv_ref, out_ref, third_ref, right_ref, grid_ref, sems):
+def grid_kernel(sizes, recv_ref, wave_ref, out_ref, side_ref, third_ref, flat_ref, mask_ref, grid_ref, right_ref, sems):
     chunks, _, width = out_ref.shape
     atoms = recv_ref.shape[2]
     blocks = width // atoms
     copies = [pltpu.make_async_copy(grid_ref.at[c], out_ref.at[c], sems.at[c]) for c in range(chunks)]
+    copies.append(pltpu.make_async_copy(right_ref, side_ref, sems.at[chunks]))
+    own_side(recv_ref, sizes, right_ref)
+    copies[chunks].start()
     for c in range(chunks):
 
         def one(place, carry):
-            fill_grid(recv_ref, c * blocks + place, place, grid_ref.at[c], third_ref, c * blocks)
+            fill_grid(recv_ref, c * blocks + place, place, grid_ref.at[c], third_ref, (0, 1), c * blocks, flat_ref)
             return carry
 
         lax.fori_loop(0, blocks, one, 0)
         copies[c].start()
-    own_side(recv_ref, sizes, right_ref)
+    mask_ref[...] = wave_mask(wave_ref)
     for copy in copies:
         copy.wait()
 
@@ -437,76 +436,78 @@
 
 
 def tiled_ewald_kernel(
-    cells,
     total_atoms,
     sizes,
     sum_ref,
     charge_ref,
     recv_ref,
     third_ref,
-    right_ref,
+    flat_ref,
+    mask_ref,
+    side_ref,
     grid_ref,
     pot_ref,
     force_ref,
     left_ref,
     prod_ref,
-    mask_ref,
     mix_ref,
     held_ref,
+    right_ref,
     sems,
 ):
-    chunks, total, width = grid_ref.shape
-    tiles, start = [], 0
-    for size in (256, 256, 512, 512):
-        tiles.append((start, size))
-        start += size
+    chunks, half, width = grid_ref.shape
+    atoms = recv_ref.shape[2]
     copies = [
-        [
-            pltpu.make_async_copy(
-                grid_ref.at[c, start : start + size, :],
-                held_ref.at[start : start + size, c * width : (c + 1) * width],
-                sems.at[number, c],
-            )
-            for c in range(chunks)
-        ]
-        for number, (start, size) in enumerate(tiles)
+        pltpu.make_async_copy(grid_ref.at[c], held_ref.at[0:half, c * width : (c + 1) * width], sems.at[c])
+        for c in range(chunks)
     ]
-    for group in copies:
-        for copy in group:
-            copy.start()
+    copies.append(pltpu.make_async_copy(side_ref, right_ref, sems.at[chunks]))
+    for copy in copies:
+        copy.start()
     make_left(sum_ref, third_ref, left_ref, charge_ref.shape[0], 0, sum_ref.shape[0])
-    for group, (start, size) in zip(copies, tiles, strict=True):
-        for copy in group:
-            copy.wait()
-        prod_ref[:, start : start + size] = dot(left_ref[...], held_ref[start : start + size, :], ((1,), (1,)))
-    apply_sums(cells, total_atoms, sizes, sum_ref, charge_ref, recv_ref, right_ref, pot_ref, force_ref, prod_ref, mask_ref, mix_ref)
+
+    def one(place, carry):
+        spot = pl.ds(pl.multiple_of(place * atoms, atoms), atoms)
+        x_sin, y_cos, y_sin = (
+            [flat_ref[24 * number + 8 * piece : 24 * number + 8 * piece + 8, spot] for piece in range(3)]
+            for number in range(3)
+        )
+        fill_products((None, x_sin), (y_cos, y_sin), (2, 3), spot, held_ref)
+        return carry
+
+    lax.fori_loop(0, sum_ref.shape[0], one, 0)
+    for copy in copies:
+        copy.wait()
+    prod_ref[...] = dot(left_ref[...], held_ref[...], ((1,), (1,)))
+    apply_sums(total_atoms, sizes, charge_ref, recv_ref, right_ref, pot_ref, force_ref, prod_ref, mask_ref, mix_ref)
 
 
 def chunked_ewald_kernel(
-    cells,
     total_atoms,
     sizes,
     sum_ref,
     charge_ref,
     recv_ref,
+    wave_ref,
     pot_ref,
     force_ref,
     left_ref,
     prod_ref,
-    mask_ref,
     mix_ref,
     grid_ref,
     third_ref,
     right_ref,
+    mask_ref,
 ):
     atoms = charge_ref.shape[1]
     chunk = grid_ref.shape[1] // atoms
     own_side(recv_ref, sizes, right_ref)
     prod_ref[...] = jnp.zeros(prod_ref.shape, f32)
+    mask_ref[...] = wave_mask(wave_ref)
 
     def whole_chunk(number, carry):
         def one(place, inner):
-            fill_grid(recv_ref, number * chunk + place, place, grid_ref, third_ref)
+            fill_grid(recv_ref, number * chunk + place, place, grid_ref, third_ref, range(4))
             return inner
 
         lax.fori_loop(0, chunk, one, 0)
@@ -520,13 +521,11 @@
         return lax.fori_loop(0, 4 * pairs // 256, tile, carry)
 
     lax.fori_loop(0, sum_ref.shape[0] // chunk, whole_chunk, 0)
-    apply_sums(cells, total_atoms, sizes, sum_ref, charge_ref, recv_ref, right_ref, pot_ref, force_ref, prod_ref, mask_ref, mix_ref)
-
-
-def apply_sums(cells, total_atoms, sizes, sum_ref, charge_ref, recv_ref, right_ref, pot_ref, force_ref, prod_ref, mask_ref, mix_ref):
+    apply_sums(total_atoms, sizes, charge_ref, recv_ref, right_ref, pot_ref, force_ref, prod_ref, mask_ref, mix_ref)
+
+
+def apply_sums(total_atoms, sizes, charge_ref, recv_ref, right_ref, pot_ref, force_ref, prod_ref, mask_ref, mix_ref):
     latent, atoms = charge_ref.shape
-    for device in range(-(-mask_rows // cells)):
-        mask_ref[device * cells : (device + 1) * cells, :] = sum_ref[device, latent : latent + cells, :].astype(f32)
     first, second = pair_values(iota((8, pairs), 1))
     flat = (first * first + second * second).astype(f32)
     for m in range(harmonics):
@@ -620,31 +619,28 @@
         out_specs=vmem(1)[0],
     )(positions, species[None, :], neighbours, ghost_rows)
     received = lax.all_to_all(outgoing, axes, 0, 0, tiled=True)
-    cells = -(-mask_rows // count)
     channels = w_in.shape[1]
     bases = radial.shape[1]
     ready = pl.pallas_call(
-        functools.partial(ready_kernel, sizes, cells),
+        ready_kernel,
         out_shape=(
             jax.ShapeDtypeStruct((2 * atoms, atoms), f32),
             jax.ShapeDtypeStruct((channels, (bases + 2) * atoms), f32),
             jax.ShapeDtypeStruct((channels, 16 * bases), f32),
             jax.ShapeDtypeStruct((3 * channels + 16, channels), bf16),
-            jax.ShapeDtypeStruct((cells, atoms), f32),
             jax.ShapeDtypeStruct((slots, atoms), i32),
         ),
-        in_specs=vmem(8),
-        out_specs=tuple(vmem(6)),
+        in_specs=vmem(7),
+        out_specs=tuple(vmem(5)),
         compiler_params=params,
-    )(neighbours, wavevectors, embedding, w_in, radial, norm_gain, w_out, w_charge.T)
-    rows_out = -(-(latent + cells) // 8) * 8
+    )(neighbours, embedding, w_in, radial, norm_gain, w_out, w_charge.T)
     outgoing, charges = pl.pallas_call(
-        functools.partial(charge_kernel, sizes, cells),
+        functools.partial(charge_kernel, sizes),
         out_shape=(
-            jax.ShapeDtypeStruct((count, rows_out, atoms), bf16),
+            jax.ShapeDtypeStruct((count, latent, atoms), bf16),
             jax.ShapeDtypeStruct((latent, atoms), f32),
         ),
-        in_specs=vmem(7),
+        in_specs=vmem(6),
         out_specs=tuple(vmem(2)),
         compiler_params=params,
     )(received, *ready)
@@ -663,42 +659,55 @@
     scratch = [
         pltpu.VMEM((rows, chunk * atoms), bf16),
         pltpu.VMEM((rows, 4 * pairs), f32),
-        pltpu.VMEM((-(-mask_rows // cells) * cells, 128), f32),
         pltpu.VMEM((rows, 4 * pairs), f32),
     ]
     if chunk < count:
         return pl.pallas_call(
-            functools.partial(chunked_ewald_kernel, cells, atoms * count, sizes),
+            functools.partial(chunked_ewald_kernel, atoms * count, sizes),
             out_shape=results,
-            in_specs=vmem(3),
+            in_specs=vmem(4),
             out_specs=tuple(vmem(2)),
-            scratch_shapes=scratch + [pltpu.VMEM(*table) for table in tables],
-        )(sums, charges, received)
+            scratch_shapes=scratch + [pltpu.VMEM(*table) for table in tables] + [pltpu.VMEM((mask_rows, 128), f32)],
+        )(sums, charges, received, wavevectors)
     chunks = count // math.gcd(count, 4)
     hbm = pl.BlockSpec(memory_space=pltpu.HBM)
-    grid, third, right = pl.pallas_call(
+    grid_shape = (chunks, 2 * pairs, count * atoms // chunks)
+    grid, side, third, flat, mask = pl.pallas_call(
         functools.partial(grid_kernel, sizes),
         out_shape=(
-            pltpu.HBM((chunks, 4 * pairs, count * atoms // chunks), bf16),
+            pltpu.HBM(grid_shape, bf16),
+            pltpu.HBM(*tables[2]),
             jax.ShapeDtypeStruct(*tables[1]),
-            jax.ShapeDtypeStruct(*tables[2]),
+            jax.ShapeDtypeStruct((72, count * atoms), f32),
+            jax.ShapeDtypeStruct((mask_rows, 128), f32),
         ),
-        in_specs=vmem(1),
-        out_specs=(hbm, *vmem(2)),
+        in_specs=vmem(2),
+        out_specs=(hbm, hbm, *vmem(3)),
         scratch_shapes=[
-            pltpu.VMEM((chunks, 4 * pairs, count * atoms // chunks), bf16),
-            pltpu.SemaphoreType.DMA((chunks,)),
+            pltpu.VMEM(grid_shape, bf16),
+            pltpu.VMEM(*tables[2]),
+            pltpu.SemaphoreType.DMA((chunks + 1,)),
         ],
         compiler_params=params,
-    )(received)
+    )(received, wavevectors)
     return pl.pallas_call(
-        functools.partial(tiled_ewald_kernel, cells, atoms * count, sizes),
+        functools.partial(tiled_ewald_kernel, atoms * count, sizes),
         out_shape=results,
-        in_specs=vmem(5) + [hbm],
+        in_specs=vmem(6) + [hbm, hbm],
         out_specs=tuple(vmem(2)),
-        scratch_shapes=scratch + [pltpu.VMEM(*tables[0]), pltpu.SemaphoreType.DMA((4, chunks))],
+        scratch_shapes=scratch
+        + [pltpu.VMEM(*tables[0]), pltpu.VMEM(*tables[2]), pltpu.SemaphoreType.DMA((chunks + 1,))],
         compiler_params=params,
-    )(sums, charges, received, third, right, pltpu.with_memory_space_constraint(grid, pltpu.HBM))
+    )(
+        sums,
+        charges,
+        received,
+        third,
+        flat,
+        mask,
+        pltpu.with_memory_space_constraint(side, pltpu.HBM),
+        pltpu.with_memory_space_constraint(grid, pltpu.HBM),
+    )
 
 
 def solution(mesh):

time: 45.1 us -> 42.2 us (0.936)
  Pallas kernels: 21.2 us -> 19.9 us
  starting transfers between devices: 11.3 us -> 10 us
  local copies, waits for them, and re-layouts: 6.03 us -> 5.11 us
  waiting for transfers between devices: 5.26 us -> 5.99 us
    all_to_all x1, waiting for transfers between devices: 1.88 us -> 3.17 us  [per_device(): received = lax.all_to_all(outgoing, axes, 0, 0, tiled=True)]
    all_to_all x1, starting transfers between devices: 3.99 us -> 2.7 us  [per_device(): sums = lax.all_to_all(outgoing, axes, 0, 0, tiled=True)]
    pallas_call x3, Pallas kernels: 14.5 us -> 13.5 us  [the longest x1 9.35 us: per_device(): pl.pallas_call(functools.partial(tiled_ewald_kernel, atoms * count, sizes...]
    unnamed x16, local copies, waits for them, and re-layouts: 6.03 us -> 5.11 us
    all_to_all x1, waiting for transfers between devices: 3.39 us -> 2.83 us  [per_device(): sums = lax.all_to_all(outgoing, axes, 0, 0, tiled=True)]
where the time goes in v3:
time: 42.2 us; the launch traced here: 41.8 us
  Pallas kernels  19.9 us (47%)
  starting transfers between devices  10 us (24%)
  waiting for transfers between devices  5.99 us (14%)
  local copies, waits for them, and re-layouts  5.11 us (12%)
  between operations  0.69 us (2%)
    pallas_call x1, Pallas kernels, per_device(): pl.pallas_call(functools.partial(tiled_ewald_kernel, atoms * count, sizes...  9.35 us
    all_to_all x1, starting transfers between devices, per_device(): received = lax.all_to_all(outgoing, axes, 0, 0, tiled=True)  7.33 us
    unnamed x16, local copies, waits for them, and re-layouts  5.11 us
    pallas_call x1, Pallas kernels, per_device(): pl.pallas_call(functools.partial(grid_kernel, sizes), out_shape=(pltpu.HB...  4.65 us
    pallas_call x1, Pallas kernels, per_device(): pl.pallas_call(functools.partial(charge_kernel, sizes), out_shape=(jax.Sh...  3.18 us
    all_to_all x1, waiting for transfers between devices, per_device(): received = lax.all_to_all(outgoing, axes, 0, 0, tiled=True)  3.17 us
    all_to_all x1, waiting for transfers between devices, per_device(): sums = lax.all_to_all(outgoing, axes, 0, 0, tiled=True)  2.83 us
    all_to_all x1, starting transfers between devices, per_device(): sums = lax.all_to_all(outgoing, axes, 0, 0, tiled=True)  2.7 us
  transfers between devices with their start and end apart: 2, of which 2 were waited for; matrix products, arithmetic and copies ran while one was open for 0% of the time, Pallas kernels for 14%

profile of v3, /device:TPU:0, one launch (start us, length us, event | category | flops | bytes accessed | tf_op | source)
XLA Modules:
  0.0 41.8 jit_solution(7258449846097636995)
XLA Ops:
  0.6 0.0 copy-start
  0.6 1.7 %shard_map.122 = bf16[32,24,128]{2,1,0:T(8,128)(2,1)} custom-call(bf16[3,128]{1,0:T(4,128)(2,1)} %pos_ref.1, s32[1,128]{1,0:T(1,128)} %bitcast.3, s32[64,128]{1,0:T(8,128)} %nbr_ref.3, s32[4,32]{1,0:T(4,128)} %rows_ref.1), custom_call_target="tpu_custom_call" | custom-call | tf_op jit(solution)/shard_map/pallas_call | solution.py:615
  2.4 7.3 %all-to-all-start = ((bf16[32,24,128]{2,1,0:T(8,128)(2,1)}), bf16[32,24,128]{2,1,0:T(8,128)(2,1)S(1)}, u32[]{:S(2)}, u32[]{:S(2)}) async-start(bf16[32,24,128]{2,1,0:T(8,128)(2,1)} %shard_map.122), calls=%async_computation | async-start | bytes 393216 | tf_op jit(solution)/shard_map/all_to_all | solution.py:621
  9.7 0.0 copy-start.1
  9.7 0.7 %copy-done.1 = s32[64,128]{1,0:T(8,128)S(1)} copy-done((s32[64,128]{1,0:T(8,128)S(1)}, s32[64,128]{1,0:T(8,128)}, u32[]{:S(2)}) %copy-start.1) | copy-done | bytes 32792
  10.5 0.0 copy-start.2
  10.5 0.8 %copy-done.2 = bf16[2,128,128]{2,1,0:T(8,128)(2,1)S(1)} copy-done((bf16[2,128,128]{2,1,0:T(8,128)(2,1)S(1)}, bf16[2,128,128]{2,1,0:T(8,128)(2,1)}, u32[]{:S(2)}) %copy-start.2) | copy-done | bytes 65560
  11.3 0.0 copy-start.3
  11.3 0.8 %copy-done.3 = bf16[2,128,128]{2,1,0:T(8,128)(2,1)S(1)} copy-done((bf16[2,128,128]{2,1,0:T(8,128)(2,1)S(1)}, bf16[2,128,128]{2,1,0:T(8,128)(2,1)}, u32[]{:S(2)}) %copy-start.3) | copy-done | bytes 65560
  12.2 0.0 copy-start.4
  12.2 0.7 %copy-done.4 = bf16[2,8,128]{2,1,0:T(8,128)(2,1)S(1)} copy-done((bf16[2,8,128]{2,1,0:T(8,128)(2,1)S(1)}, bf16[2,8,128]{2,1,0:T(8,128)(2,1)}, u32[]{:S(2)}) %copy-start.4) | copy-done | bytes 4120
  12.9 0.0 copy-start.5
  12.9 0.7 %copy-done.5 = bf16[128,8]{0,1:T(8,128)(2,1)S(1)} copy-done((bf16[128,8]{0,1:T(8,128)(2,1)S(1)}, bf16[128,8]{0,1:T(8,128)(2,1)}, u32[]{:S(2)}) %copy-start.5) | copy-done | bytes 2072
  13.5 0.0 copy-start.6
  13.5 0.7 %copy-done.6 = bf16[2,128]{1,0:T(2,128)(2,1)S(1)} copy-done((bf16[2,128]{1,0:T(2,128)(2,1)S(1)}, bf16[2,128]{1,0:T(2,128)(2,1)}, u32[]{:S(2)}) %copy-start.6) | copy-done | bytes 536
  14.2 0.7 %copy-done.7 = bf16[2,128]{1,0:T(2,128)(2,1)S(1)} copy-done((bf16[2,128]{1,0:T(2,128)(2,1)S(1)}, bf16[2,128]{1,0:T(2,128)(2,1)}, u32[]{:S(2)}) %copy-start.7) | copy-done | bytes 536
  14.8 1.0 %shard_map.123 = (f32[256,128]{1,0:T(8,128)S(1)}, f32[128,1280]{1,0:T(8,128)S(1)}, f32[128,128]{1,0:T(8,128)S(1)}, bf16[400,128]{1,0:T(8,128)(2,1)S(1)}, s32[64,128]{1,0:T(8,128)S(1)}) custom-call(s32[64,128]{1,0:T(8,128)S(1)} %copy-done.1, bf16[2,128]{1,0:T(2,128)(2,1)S(1)} %copy-done.6, bf16[2,128,128]{2,1,0:T(8,128)(2,1)S(1)} %copy-done.2, ...), custom_call_target="tpu_custom_call" | custom-call | tf_op jit(solution)/shard_map/pallas_call | solution.py:624
  15.9 3.2 %all-to-all-done.recv_ref = bf16[32,24,128]{2,1,0:T(8,128)(2,1)S(1)} async-done(((bf16[32,24,128]{2,1,0:T(8,128)(2,1)}), bf16[32,24,128]{2,1,0:T(8,128)(2,1)S(1)}, u32[]{:S(2)}, u32[]{:S(2)}) %all-to-all-start) | async-done | bytes 196640 | tf_op jit(solution)/shard_map/all_to_all | solution.py:621
  19.0 3.2 %shard_map.124 = (bf16[32,8,128]{2,1,0:T(8,128)(2,1)}, f32[8,128]{1,0:T(8,128)S(1)}) custom-call(bf16[32,24,128]{2,1,0:T(8,128)(2,1)S(1)} %all-to-all-done.recv_ref, f32[256,128]{1,0:T(8,128)S(1)} %get-tuple-element.14.times_ref, f32[128,1280]{1,0:T(8,128)S(1)} %get-tuple-element.15.column_ref, f32[128,128]{1,0:T(8,128)S(1)} %get-tuple-element.16.weight_ref, ...), custom_call_target="tpu_custom_call" | custom-call | tf_op jit(solution)/shard_map/pallas_call | solution.py:637
  22.2 2.7 %all-to-all-start.1 = ((bf16[32,8,128]{2,1,0:T(8,128)(2,1)}), bf16[32,8,128]{2,1,0:T(8,128)(2,1)S(1)}, u32[]{:S(2)}, u32[]{:S(2)}) async-start(bf16[32,8,128]{2,1,0:T(8,128)(2,1)} %get-tuple-element.19), calls=%async_computation.1 | async-start | bytes 131072 | tf_op jit(solution)/shard_map/all_to_all | solution.py:647
  24.9 0.0 copy-done
  24.9 4.7 %shard_map.125 = (bf16[8,768,512]{2,1,0:T(8,128)(2,1)}, bf16[1536,384]{1,0:T(8,128)(2,1)}, f32[48,4096]{1,0:T(8,128)S(1)}, f32[72,4096]{1,0:T(8,128)S(1)}, f32[240,128]{1,0:T(8,128)S(1)}) custom-call(bf16[32,24,128]{2,1,0:T(8,128)(2,1)S(1)} %all-to-all-done.recv_ref, s32[3,12288]{1,0:T(4,128)S(1)} %copy-done), custom_call_target="tpu_custom_call" | custom-call | tf_op jit(solution)/shard_map/pallas_call | solution.py:675
  29.6 2.8 %all-to-all-done.1.sum_ref = bf16[32,8,128]{2,1,0:T(8,128)(2,1)S(1)} async-done(((bf16[32,8,128]{2,1,0:T(8,128)(2,1)}), bf16[32,8,128]{2,1,0:T(8,128)(2,1)S(1)}, u32[]{:S(2)}, u32[]{:S(2)}) %all-to-all-start.1) | async-done | bytes 65568 | tf_op jit(solution)/shard_map/all_to_all | solution.py:647
  32.4 9.4 %shard_map.126 = (f32[8,128]{1,0:T(8,128)}, f32[3,128]{1,0:T(4,128)}) custom-call(bf16[32,8,128]{2,1,0:T(8,128)(2,1)S(1)} %all-to-all-done.1.sum_ref, f32[8,128]{1,0:T(8,128)S(1)} %get-tuple-element.20.charge_ref, bf16[32,24,128]{2,1,0:T(8,128)(2,1)S(1)} %all-to-all-done.recv_ref, f32[48,4096]{1,0:T(8,128)S(1)} %get-tuple-element.21.third_ref, ...), custom_call_target="tpu_custom_call" | custom-call | tf_op jit(solution)/shard_map/pallas_call | solution.py:693
  (1 shorter events, 0.0 us)
Async XLA Ops:
  0.6 24.3 %copy-start = (s32[3,12288]{1,0:T(4,128)S(1)}, s32[3,12288]{1,0:T(4,128)}, u32[]{:S(2)}) copy-start(s32[3,12288]{1,0:T(4,128)} %wave_ref.1) | copy-start | bytes 442372
  2.4 16.6 %all-to-all-start = ((bf16[32,24,128]{2,1,0:T(8,128)(2,1)}), bf16[32,24,128]{2,1,0:T(8,128)(2,1)S(1)}, u32[]{:S(2)}, u32[]{:S(2)}) async-start(bf16[32,24,128]{2,1,0:T(8,128)(2,1)} %shard_map.122), calls=%async_computation | async-start | bytes 393216 | tf_op jit(solution)/shard_map/all_to_all | solution.py:621
  9.7 0.8 %copy-start.1 = (s32[64,128]{1,0:T(8,128)S(1)}, s32[64,128]{1,0:T(8,128)}, u32[]{:S(2)}) copy-start(s32[64,128]{1,0:T(8,128)} %nbr_ref.3) | copy-start | bytes 98308
  10.5 0.8 %copy-start.2 = (bf16[2,128,128]{2,1,0:T(8,128)(2,1)S(1)}, bf16[2,128,128]{2,1,0:T(8,128)(2,1)}, u32[]{:S(2)}) copy-start(bf16[2,128,128]{2,1,0:T(8,128)(2,1)} %w_in_ref.1) | copy-start | bytes 196612
  11.3 0.8 %copy-start.3 = (bf16[2,128,128]{2,1,0:T(8,128)(2,1)S(1)}, bf16[2,128,128]{2,1,0:T(8,128)(2,1)}, u32[]{:S(2)}) copy-start(bf16[2,128,128]{2,1,0:T(8,128)(2,1)} %w_out_ref.1) | copy-start | bytes 196612
  12.2 0.7 %copy-start.4 = (bf16[2,8,128]{2,1,0:T(8,128)(2,1)S(1)}, bf16[2,8,128]{2,1,0:T(8,128)(2,1)}, u32[]{:S(2)}) copy-start(bf16[2,8,128]{2,1,0:T(8,128)(2,1)} %radial_ref.1) | copy-start | bytes 12292
  12.9 0.7 %copy-start.5 = (bf16[128,8]{0,1:T(8,128)(2,1)S(1)}, bf16[128,8]{0,1:T(8,128)(2,1)}, u32[]{:S(2)}) copy-start(bf16[128,8]{0,1:T(8,128)(2,1)} %param.21) | copy-start | bytes 6148
  13.5 0.7 %copy-start.6 = (bf16[2,128]{1,0:T(2,128)(2,1)S(1)}, bf16[2,128]{1,0:T(2,128)(2,1)}, u32[]{:S(2)}) copy-start(bf16[2,128]{1,0:T(2,128)(2,1)} %emb_ref.1) | copy-start | bytes 1540
  14.2 0.7 %copy-start.7 = (bf16[2,128]{1,0:T(2,128)(2,1)S(1)}, bf16[2,128]{1,0:T(2,128)(2,1)}, u32[]{:S(2)}) copy-start(bf16[2,128]{1,0:T(2,128)(2,1)} %gain_ref.1) | copy-start | bytes 1540
  22.2 10.2 %all-to-all-start.1 = ((bf16[32,8,128]{2,1,0:T(8,128)(2,1)}), bf16[32,8,128]{2,1,0:T(8,128)(2,1)S(1)}, u32[]{:S(2)}, u32[]{:S(2)}) async-start(bf16[32,8,128]{2,1,0:T(8,128)(2,1)} %get-tuple-element.19), calls=%async_computation.1 | async-start | bytes 131072 | tf_op jit(solution)/shard_map/all_to_all | solution.py:647

commit v4 on v3

--- a/solution.py
+++ b/solution.py
@@ -418,21 +418,14 @@
         copy.wait()
 
 
-def make_left(sum_ref, third_ref, left_ref, latent, first_device, chunk):
-    atoms = sum_ref.shape[2]
-
-    def one(place, inner):
-        spot = pl.ds(pl.multiple_of(place * atoms, atoms), atoms)
-        charge = sum_ref[first_device + place, 0:latent, :].astype(f32)
-        left = []
-        for kind in range(2):
-            for m in range(harmonics):
-                left.append(charge * jnp.broadcast_to(third_ref[24 * kind + m : 24 * kind + m + 1, spot], (latent, atoms)))
-        for at in range(0, 2 * harmonics, 2):
-            left_ref[at * latent : (at + 2) * latent, spot] = jnp.concatenate(left[at : at + 2], axis=0).astype(bf16)
-        return inner
-
-    lax.fori_loop(0, chunk, one, 0)
+def left_rows(sum_ref, third_ref, left_ref, latent, device, spot):
+    charge = sum_ref[device, 0:latent, :].astype(f32)
+    left = []
+    for kind in range(2):
+        for m in range(harmonics):
+            left.append(charge * jnp.broadcast_to(third_ref[24 * kind + m : 24 * kind + m + 1, spot], charge.shape))
+    for at in range(0, 2 * harmonics, 2):
+        left_ref[at * latent : (at + 2) * latent, spot] = jnp.concatenate(left[at : at + 2], axis=0).astype(bf16)
 
 
 def tiled_ewald_kernel(
@@ -462,23 +455,29 @@
         for c in range(chunks)
     ]
     copies.append(pltpu.make_async_copy(side_ref, right_ref, sems.at[chunks]))
-    for copy in copies:
+    for copy in copies[:chunks]:
         copy.start()
-    make_left(sum_ref, third_ref, left_ref, charge_ref.shape[0], 0, sum_ref.shape[0])
-
-    def one(place, carry):
-        spot = pl.ds(pl.multiple_of(place * atoms, atoms), atoms)
-        x_sin, y_cos, y_sin = (
-            [flat_ref[24 * number + 8 * piece : 24 * number + 8 * piece + 8, spot] for piece in range(3)]
-            for number in range(3)
-        )
-        fill_products((None, x_sin), (y_cos, y_sin), (2, 3), spot, held_ref)
+    latent = charge_ref.shape[0]
+    unroll = math.gcd(sum_ref.shape[0], 2)
+
+    def some(step, carry):
+        for part in range(unroll):
+            place = step * unroll + part
+            spot = pl.ds(pl.multiple_of(place * atoms, atoms), atoms)
+            left_rows(sum_ref, third_ref, left_ref, latent, place, spot)
+            x_sin, y_cos, y_sin = (
+                [flat_ref[24 * number + 8 * piece : 24 * number + 8 * piece + 8, spot] for piece in range(3)]
+                for number in range(3)
+            )
+            fill_products((None, x_sin), (y_cos, y_sin), (2, 3), spot, held_ref)
         return carry
 
-    lax.fori_loop(0, sum_ref.shape[0], one, 0)
-    for copy in copies:
+    lax.fori_loop(0, sum_ref.shape[0] // unroll, some, 0)
+    for copy in copies[:chunks]:
         copy.wait()
+    copies[chunks].start()
     prod_ref[...] = dot(left_ref[...], held_ref[...], ((1,), (1,)))
+    copies[chunks].wait()
     apply_sums(total_atoms, sizes, charge_ref, recv_ref, right_ref, pot_ref, force_ref, prod_ref, mask_ref, mix_ref)
 
 
@@ -508,10 +507,11 @@
     def whole_chunk(number, carry):
         def one(place, inner):
             fill_grid(recv_ref, number * chunk + place, place, grid_ref, third_ref, range(4))
+            spot = pl.ds(pl.multiple_of(place * atoms, atoms), atoms)
+            left_rows(sum_ref, third_ref, left_ref, charge_ref.shape[0], number * chunk + place, spot)
             return inner
 
         lax.fori_loop(0, chunk, one, 0)
-        make_left(sum_ref, third_ref, left_ref, charge_ref.shape[0], number * chunk, chunk)
 
         def tile(column, inner):
             spot = pl.ds(pl.multiple_of(column * 256, 256), 256)

time: 42.2 us -> 42 us (level)
  no operation moved by 1% of the time
where the time goes in v4:
time: 42 us; the launch traced here: 41.6 us
  Pallas kernels  19.7 us (47%)
  starting transfers between devices  10 us (24%)
  waiting for transfers between devices  5.99 us (14%)
  local copies, waits for them, and re-layouts  5.11 us (12%)
  between operations  0.69 us (2%)
    pallas_call x1, Pallas kernels, per_device(): pl.pallas_call(functools.partial(tiled_ewald_kernel, atoms * count, sizes...  9.15 us
    all_to_all x1, starting transfers between devices, per_device(): received = lax.all_to_all(outgoing, axes, 0, 0, tiled=True)  7.33 us
    unnamed x16, local copies, waits for them, and re-layouts  5.11 us
    pallas_call x1, Pallas kernels, per_device(): pl.pallas_call(functools.partial(grid_kernel, sizes), out_shape=(pltpu.HB...  4.65 us
    pallas_call x1, Pallas kernels, per_device(): pl.pallas_call(functools.partial(charge_kernel, sizes), out_shape=(jax.Sh...  3.18 us
    all_to_all x1, waiting for transfers between devices, per_device(): received = lax.all_to_all(outgoing, axes, 0, 0, tiled=True)  3.17 us
    all_to_all x1, waiting for transfers between devices, per_device(): sums = lax.all_to_all(outgoing, axes, 0, 0, tiled=True)  2.83 us
    all_to_all x1, starting transfers between devices, per_device(): sums = lax.all_to_all(outgoing, axes, 0, 0, tiled=True)  2.7 us
  transfers between devices with their start and end apart: 2, of which 2 were waited for; matrix products, arithmetic and copies ran while one was open for 0% of the time, Pallas kernels for 14%

profile of v4, /device:TPU:0, one launch (start us, length us, event | category | flops | bytes accessed | tf_op | source)
XLA Modules:
  0.0 41.6 jit_solution(2795914419621232008)
XLA Ops:
  0.6 0.0 copy-start
  0.6 1.7 %shard_map.122 = bf16[32,24,128]{2,1,0:T(8,128)(2,1)} custom-call(bf16[3,128]{1,0:T(4,128)(2,1)} %pos_ref.1, s32[1,128]{1,0:T(1,128)} %bitcast.3, s32[64,128]{1,0:T(8,128)} %nbr_ref.3, s32[4,32]{1,0:T(4,128)} %rows_ref.1), custom_call_target="tpu_custom_call" | custom-call | tf_op jit(solution)/shard_map/pallas_call | solution.py:615
  2.4 7.3 %all-to-all-start = ((bf16[32,24,128]{2,1,0:T(8,128)(2,1)}), bf16[32,24,128]{2,1,0:T(8,128)(2,1)S(1)}, u32[]{:S(2)}, u32[]{:S(2)}) async-start(bf16[32,24,128]{2,1,0:T(8,128)(2,1)} %shard_map.122), calls=%async_computation | async-start | bytes 393216 | tf_op jit(solution)/shard_map/all_to_all | solution.py:621
  9.7 0.0 copy-start.1
  9.7 0.7 %copy-done.1 = s32[64,128]{1,0:T(8,128)S(1)} copy-done((s32[64,128]{1,0:T(8,128)S(1)}, s32[64,128]{1,0:T(8,128)}, u32[]{:S(2)}) %copy-start.1) | copy-done | bytes 32792
  10.5 0.0 copy-start.2
  10.5 0.8 %copy-done.2 = bf16[2,128,128]{2,1,0:T(8,128)(2,1)S(1)} copy-done((bf16[2,128,128]{2,1,0:T(8,128)(2,1)S(1)}, bf16[2,128,128]{2,1,0:T(8,128)(2,1)}, u32[]{:S(2)}) %copy-start.2) | copy-done | bytes 65560
  11.3 0.0 copy-start.3
  11.3 0.8 %copy-done.3 = bf16[2,128,128]{2,1,0:T(8,128)(2,1)S(1)} copy-done((bf16[2,128,128]{2,1,0:T(8,128)(2,1)S(1)}, bf16[2,128,128]{2,1,0:T(8,128)(2,1)}, u32[]{:S(2)}) %copy-start.3) | copy-done | bytes 65560
  12.2 0.0 copy-start.4
  12.2 0.7 %copy-done.4 = bf16[2,8,128]{2,1,0:T(8,128)(2,1)S(1)} copy-done((bf16[2,8,128]{2,1,0:T(8,128)(2,1)S(1)}, bf16[2,8,128]{2,1,0:T(8,128)(2,1)}, u32[]{:S(2)}) %copy-start.4) | copy-done | bytes 4120
  12.9 0.0 copy-start.5
  12.9 0.7 %copy-done.5 = bf16[128,8]{0,1:T(8,128)(2,1)S(1)} copy-done((bf16[128,8]{0,1:T(8,128)(2,1)S(1)}, bf16[128,8]{0,1:T(8,128)(2,1)}, u32[]{:S(2)}) %copy-start.5) | copy-done | bytes 2072
  13.5 0.0 copy-start.6
  13.5 0.7 %copy-done.6 = bf16[2,128]{1,0:T(2,128)(2,1)S(1)} copy-done((bf16[2,128]{1,0:T(2,128)(2,1)S(1)}, bf16[2,128]{1,0:T(2,128)(2,1)}, u32[]{:S(2)}) %copy-start.6) | copy-done | bytes 536
  14.2 0.7 %copy-done.7 = bf16[2,128]{1,0:T(2,128)(2,1)S(1)} copy-done((bf16[2,128]{1,0:T(2,128)(2,1)S(1)}, bf16[2,128]{1,0:T(2,128)(2,1)}, u32[]{:S(2)}) %copy-start.7) | copy-done | bytes 536
  14.8 1.0 %shard_map.123 = (f32[256,128]{1,0:T(8,128)S(1)}, f32[128,1280]{1,0:T(8,128)S(1)}, f32[128,128]{1,0:T(8,128)S(1)}, bf16[400,128]{1,0:T(8,128)(2,1)S(1)}, s32[64,128]{1,0:T(8,128)S(1)}) custom-call(s32[64,128]{1,0:T(8,128)S(1)} %copy-done.1, bf16[2,128]{1,0:T(2,128)(2,1)S(1)} %copy-done.6, bf16[2,128,128]{2,1,0:T(8,128)(2,1)S(1)} %copy-done.2, ...), custom_call_target="tpu_custom_call" | custom-call | tf_op jit(solution)/shard_map/pallas_call | solution.py:624
  15.9 3.2 %all-to-all-done.recv_ref = bf16[32,24,128]{2,1,0:T(8,128)(2,1)S(1)} async-done(((bf16[32,24,128]{2,1,0:T(8,128)(2,1)}), bf16[32,24,128]{2,1,0:T(8,128)(2,1)S(1)}, u32[]{:S(2)}, u32[]{:S(2)}) %all-to-all-start) | async-done | bytes 196640 | tf_op jit(solution)/shard_map/all_to_all | solution.py:621
  19.0 3.2 %shard_map.124 = (bf16[32,8,128]{2,1,0:T(8,128)(2,1)}, f32[8,128]{1,0:T(8,128)S(1)}) custom-call(bf16[32,24,128]{2,1,0:T(8,128)(2,1)S(1)} %all-to-all-done.recv_ref, f32[256,128]{1,0:T(8,128)S(1)} %get-tuple-element.14.times_ref, f32[128,1280]{1,0:T(8,128)S(1)} %get-tuple-element.15.column_ref, f32[128,128]{1,0:T(8,128)S(1)} %get-tuple-element.16.weight_ref, ...), custom_call_target="tpu_custom_call" | custom-call | tf_op jit(solution)/shard_map/pallas_call | solution.py:637
  22.2 2.7 %all-to-all-start.1 = ((bf16[32,8,128]{2,1,0:T(8,128)(2,1)}), bf16[32,8,128]{2,1,0:T(8,128)(2,1)S(1)}, u32[]{:S(2)}, u32[]{:S(2)}) async-start(bf16[32,8,128]{2,1,0:T(8,128)(2,1)} %get-tuple-element.19), calls=%async_computation.1 | async-start | bytes 131072 | tf_op jit(solution)/shard_map/all_to_all | solution.py:647
  24.9 0.0 copy-done
  24.9 4.7 %shard_map.125 = (bf16[8,768,512]{2,1,0:T(8,128)(2,1)}, bf16[1536,384]{1,0:T(8,128)(2,1)}, f32[48,4096]{1,0:T(8,128)S(1)}, f32[72,4096]{1,0:T(8,128)S(1)}, f32[240,128]{1,0:T(8,128)S(1)}) custom-call(bf16[32,24,128]{2,1,0:T(8,128)(2,1)S(1)} %all-to-all-done.recv_ref, s32[3,12288]{1,0:T(4,128)S(1)} %copy-done), custom_call_target="tpu_custom_call" | custom-call | tf_op jit(solution)/shard_map/pallas_call | solution.py:675
  29.6 2.8 %all-to-all-done.1.sum_ref = bf16[32,8,128]{2,1,0:T(8,128)(2,1)S(1)} async-done(((bf16[32,8,128]{2,1,0:T(8,128)(2,1)}), bf16[32,8,128]{2,1,0:T(8,128)(2,1)S(1)}, u32[]{:S(2)}, u32[]{:S(2)}) %all-to-all-start.1) | async-done | bytes 65568 | tf_op jit(solution)/shard_map/all_to_all | solution.py:647
  32.4 9.2 %shard_map.126 = (f32[8,128]{1,0:T(8,128)}, f32[3,128]{1,0:T(4,128)}) custom-call(bf16[32,8,128]{2,1,0:T(8,128)(2,1)S(1)} %all-to-all-done.1.sum_ref, f32[8,128]{1,0:T(8,128)S(1)} %get-tuple-element.20.charge_ref, bf16[32,24,128]{2,1,0:T(8,128)(2,1)S(1)} %all-to-all-done.recv_ref, f32[48,4096]{1,0:T(8,128)S(1)} %get-tuple-element.21.third_ref, ...), custom_call_target="tpu_custom_call" | custom-call | tf_op jit(solution)/shard_map/pallas_call | solution.py:693
  (1 shorter events, 0.0 us)
Async XLA Ops:
  0.6 24.3 %copy-start = (s32[3,12288]{1,0:T(4,128)S(1)}, s32[3,12288]{1,0:T(4,128)}, u32[]{:S(2)}) copy-start(s32[3,12288]{1,0:T(4,128)} %wave_ref.1) | copy-start | bytes 442372
  2.4 16.6 %all-to-all-start = ((bf16[32,24,128]{2,1,0:T(8,128)(2,1)}), bf16[32,24,128]{2,1,0:T(8,128)(2,1)S(1)}, u32[]{:S(2)}, u32[]{:S(2)}) async-start(bf16[32,24,128]{2,1,0:T(8,128)(2,1)} %shard_map.122), calls=%async_computation | async-start | bytes 393216 | tf_op jit(solution)/shard_map/all_to_all | solution.py:621
  9.7 0.8 %copy-start.1 = (s32[64,128]{1,0:T(8,128)S(1)}, s32[64,128]{1,0:T(8,128)}, u32[]{:S(2)}) copy-start(s32[64,128]{1,0:T(8,128)} %nbr_ref.3) | copy-start | bytes 98308
  10.5 0.8 %copy-start.2 = (bf16[2,128,128]{2,1,0:T(8,128)(2,1)S(1)}, bf16[2,128,128]{2,1,0:T(8,128)(2,1)}, u32[]{:S(2)}) copy-start(bf16[2,128,128]{2,1,0:T(8,128)(2,1)} %w_in_ref.1) | copy-start | bytes 196612
  11.3 0.8 %copy-start.3 = (bf16[2,128,128]{2,1,0:T(8,128)(2,1)S(1)}, bf16[2,128,128]{2,1,0:T(8,128)(2,1)}, u32[]{:S(2)}) copy-start(bf16[2,128,128]{2,1,0:T(8,128)(2,1)} %w_out_ref.1) | copy-start | bytes 196612
  12.2 0.7 %copy-start.4 = (bf16[2,8,128]{2,1,0:T(8,128)(2,1)S(1)}, bf16[2,8,128]{2,1,0:T(8,128)(2,1)}, u32[]{:S(2)}) copy-start(bf16[2,8,128]{2,1,0:T(8,128)(2,1)} %radial_ref.1) | copy-start | bytes 12292
  12.9 0.7 %copy-start.5 = (bf16[128,8]{0,1:T(8,128)(2,1)S(1)}, bf16[128,8]{0,1:T(8,128)(2,1)}, u32[]{:S(2)}) copy-start(bf16[128,8]{0,1:T(8,128)(2,1)} %param.21) | copy-start | bytes 6148
  13.5 0.7 %copy-start.6 = (bf16[2,128]{1,0:T(2,128)(2,1)S(1)}, bf16[2,128]{1,0:T(2,128)(2,1)}, u32[]{:S(2)}) copy-start(bf16[2,128]{1,0:T(2,128)(2,1)} %emb_ref.1) | copy-start | bytes 1540
  14.2 0.7 %copy-start.7 = (bf16[2,128]{1,0:T(2,128)(2,1)S(1)}, bf16[2,128]{1,0:T(2,128)(2,1)}, u32[]{:S(2)}) copy-start(bf16[2,128]{1,0:T(2,128)(2,1)} %gain_ref.1) | copy-start | bytes 1540
  22.2 10.2 %all-to-all-start.1 = ((bf16[32,8,128]{2,1,0:T(8,128)(2,1)}), bf16[32,8,128]{2,1,0:T(8,128)(2,1)S(1)}, u32[]{:S(2)}, u32[]{:S(2)}) async-start(bf16[32,8,128]{2,1,0:T(8,128)(2,1)} %get-tuple-element.19), calls=%async_computation.1 | async-start | bytes 131072 | tf_op jit(solution)/shard_map/all_to_all | solution.py:647

commit v5 on v4

--- a/solution.py
+++ b/solution.py
@@ -669,7 +669,7 @@
             out_specs=tuple(vmem(2)),
             scratch_shapes=scratch + [pltpu.VMEM(*table) for table in tables] + [pltpu.VMEM((mask_rows, 128), f32)],
         )(sums, charges, received, wavevectors)
-    chunks = count // math.gcd(count, 4)
+    chunks = count // math.gcd(count, 8)
     hbm = pl.BlockSpec(memory_space=pltpu.HBM)
     grid_shape = (chunks, 2 * pairs, count * atoms // chunks)
     grid, side, third, flat, mask = pl.pallas_call(

time: 42 us -> 42 us (level)
  waiting for transfers between devices: 5.99 us -> 5.07 us
  Pallas kernels: 19.7 us -> 20.6 us
    all_to_all x1, waiting for transfers between devices: 2.83 us -> 1.91 us  [per_device(): sums = lax.all_to_all(outgoing, axes, 0, 0, tiled=True)]
    pallas_call x1, Pallas kernels: 4.65 us -> 5.57 us  [per_device(): pl.pallas_call(functools.partial(grid_kernel, sizes), out_shape=(pltpu.HB...]
  transfers between devices with their start and end apart: 2 -> 2, of which waited for: 2 -> 2; matrix products, arithmetic and copies ran while one was open for 0% -> 0% of each run, Pallas kernels for 14% -> 16%
where the time goes in v5:
time: 42 us; the launch traced here: 41.5 us
  Pallas kernels  20.6 us (49%)
  starting transfers between devices  10 us (24%)
  local copies, waits for them, and re-layouts  5.11 us (12%)
  waiting for transfers between devices  5.07 us (12%)
  between operations  0.69 us (2%)
    pallas_call x1, Pallas kernels, per_device(): pl.pallas_call(functools.partial(tiled_ewald_kernel, atoms * count, sizes...  9.11 us
    all_to_all x1, starting transfers between devices, per_device(): received = lax.all_to_all(outgoing, axes, 0, 0, tiled=True)  7.33 us
    pallas_call x1, Pallas kernels, per_device(): pl.pallas_call(functools.partial(grid_kernel, sizes), out_shape=(pltpu.HB...  5.57 us
    unnamed x16, local copies, waits for them, and re-layouts  5.11 us
    pallas_call x1, Pallas kernels, per_device(): pl.pallas_call(functools.partial(charge_kernel, sizes), out_shape=(jax.Sh...  3.18 us
    all_to_all x1, waiting for transfers between devices, per_device(): received = lax.all_to_all(outgoing, axes, 0, 0, tiled=True)  3.17 us
    all_to_all x1, starting transfers between devices, per_device(): sums = lax.all_to_all(outgoing, axes, 0, 0, tiled=True)  2.7 us
    all_to_all x1, waiting for transfers between devices, per_device(): sums = lax.all_to_all(outgoing, axes, 0, 0, tiled=True)  1.91 us
  transfers between devices with their start and end apart: 2, of which 2 were waited for; matrix products, arithmetic and copies ran while one was open for 0% of the time, Pallas kernels for 16%

profile of v5, /device:TPU:0, one launch (start us, length us, event | category | flops | bytes accessed | tf_op | source)
XLA Modules:
  0.0 41.5 jit_solution(13536129443788731826)
XLA Ops:
  0.6 0.0 copy-start
  0.6 1.7 %shard_map.122 = bf16[32,24,128]{2,1,0:T(8,128)(2,1)} custom-call(bf16[3,128]{1,0:T(4,128)(2,1)} %pos_ref.1, s32[1,128]{1,0:T(1,128)} %bitcast.3, s32[64,128]{1,0:T(8,128)} %nbr_ref.3, s32[4,32]{1,0:T(4,128)} %rows_ref.1), custom_call_target="tpu_custom_call" | custom-call | tf_op jit(solution)/shard_map/pallas_call | solution.py:615
  2.4 7.3 %all-to-all-start = ((bf16[32,24,128]{2,1,0:T(8,128)(2,1)}), bf16[32,24,128]{2,1,0:T(8,128)(2,1)S(1)}, u32[]{:S(2)}, u32[]{:S(2)}) async-start(bf16[32,24,128]{2,1,0:T(8,128)(2,1)} %shard_map.122), calls=%async_computation | async-start | bytes 393216 | tf_op jit(solution)/shard_map/all_to_all | solution.py:621
  9.7 0.0 copy-start.1
  9.7 0.7 %copy-done.1 = s32[64,128]{1,0:T(8,128)S(1)} copy-done((s32[64,128]{1,0:T(8,128)S(1)}, s32[64,128]{1,0:T(8,128)}, u32[]{:S(2)}) %copy-start.1) | copy-done | bytes 32792
  10.5 0.0 copy-start.2
  10.5 0.8 %copy-done.2 = bf16[2,128,128]{2,1,0:T(8,128)(2,1)S(1)} copy-done((bf16[2,128,128]{2,1,0:T(8,128)(2,1)S(1)}, bf16[2,128,128]{2,1,0:T(8,128)(2,1)}, u32[]{:S(2)}) %copy-start.2) | copy-done | bytes 65560
  11.3 0.0 copy-start.3
  11.3 0.8 %copy-done.3 = bf16[2,128,128]{2,1,0:T(8,128)(2,1)S(1)} copy-done((bf16[2,128,128]{2,1,0:T(8,128)(2,1)S(1)}, bf16[2,128,128]{2,1,0:T(8,128)(2,1)}, u32[]{:S(2)}) %copy-start.3) | copy-done | bytes 65560
  12.2 0.0 copy-start.4
  12.2 0.7 %copy-done.4 = bf16[2,8,128]{2,1,0:T(8,128)(2,1)S(1)} copy-done((bf16[2,8,128]{2,1,0:T(8,128)(2,1)S(1)}, bf16[2,8,128]{2,1,0:T(8,128)(2,1)}, u32[]{:S(2)}) %copy-start.4) | copy-done | bytes 4120
  12.9 0.0 copy-start.5
  12.9 0.7 %copy-done.5 = bf16[128,8]{0,1:T(8,128)(2,1)S(1)} copy-done((bf16[128,8]{0,1:T(8,128)(2,1)S(1)}, bf16[128,8]{0,1:T(8,128)(2,1)}, u32[]{:S(2)}) %copy-start.5) | copy-done | bytes 2072
  13.5 0.0 copy-start.6
  13.5 0.7 %copy-done.6 = bf16[2,128]{1,0:T(2,128)(2,1)S(1)} copy-done((bf16[2,128]{1,0:T(2,128)(2,1)S(1)}, bf16[2,128]{1,0:T(2,128)(2,1)}, u32[]{:S(2)}) %copy-start.6) | copy-done | bytes 536
  14.2 0.7 %copy-done.7 = bf16[2,128]{1,0:T(2,128)(2,1)S(1)} copy-done((bf16[2,128]{1,0:T(2,128)(2,1)S(1)}, bf16[2,128]{1,0:T(2,128)(2,1)}, u32[]{:S(2)}) %copy-start.7) | copy-done | bytes 536
  14.8 1.0 %shard_map.123 = (f32[256,128]{1,0:T(8,128)S(1)}, f32[128,1280]{1,0:T(8,128)S(1)}, f32[128,128]{1,0:T(8,128)S(1)}, bf16[400,128]{1,0:T(8,128)(2,1)S(1)}, s32[64,128]{1,0:T(8,128)S(1)}) custom-call(s32[64,128]{1,0:T(8,128)S(1)} %copy-done.1, bf16[2,128]{1,0:T(2,128)(2,1)S(1)} %copy-done.6, bf16[2,128,128]{2,1,0:T(8,128)(2,1)S(1)} %copy-done.2, ...), custom_call_target="tpu_custom_call" | custom-call | tf_op jit(solution)/shard_map/pallas_call | solution.py:624
  15.9 3.2 %all-to-all-done.recv_ref = bf16[32,24,128]{2,1,0:T(8,128)(2,1)S(1)} async-done(((bf16[32,24,128]{2,1,0:T(8,128)(2,1)}), bf16[32,24,128]{2,1,0:T(8,128)(2,1)S(1)}, u32[]{:S(2)}, u32[]{:S(2)}) %all-to-all-start) | async-done | bytes 196640 | tf_op jit(solution)/shard_map/all_to_all | solution.py:621
  19.0 3.2 %shard_map.124 = (bf16[32,8,128]{2,1,0:T(8,128)(2,1)}, f32[8,128]{1,0:T(8,128)S(1)}) custom-call(bf16[32,24,128]{2,1,0:T(8,128)(2,1)S(1)} %all-to-all-done.recv_ref, f32[256,128]{1,0:T(8,128)S(1)} %get-tuple-element.14.times_ref, f32[128,1280]{1,0:T(8,128)S(1)} %get-tuple-element.15.column_ref, f32[128,128]{1,0:T(8,128)S(1)} %get-tuple-element.16.weight_ref, ...), custom_call_target="tpu_custom_call" | custom-call | tf_op jit(solution)/shard_map/pallas_call | solution.py:637
  22.2 2.7 %all-to-all-start.1 = ((bf16[32,8,128]{2,1,0:T(8,128)(2,1)}), bf16[32,8,128]{2,1,0:T(8,128)(2,1)S(1)}, u32[]{:S(2)}, u32[]{:S(2)}) async-start(bf16[32,8,128]{2,1,0:T(8,128)(2,1)} %get-tuple-element.19), calls=%async_computation.1 | async-start | bytes 131072 | tf_op jit(solution)/shard_map/all_to_all | solution.py:647
  24.9 0.0 copy-done
  24.9 5.6 %shard_map.125 = (bf16[4,768,1024]{2,1,0:T(8,128)(2,1)}, bf16[1536,384]{1,0:T(8,128)(2,1)}, f32[48,4096]{1,0:T(8,128)S(1)}, f32[72,4096]{1,0:T(8,128)S(1)}, f32[240,128]{1,0:T(8,128)S(1)}) custom-call(bf16[32,24,128]{2,1,0:T(8,128)(2,1)S(1)} %all-to-all-done.recv_ref, s32[3,12288]{1,0:T(4,128)S(1)} %copy-done), custom_call_target="tpu_custom_call" | custom-call | tf_op jit(solution)/shard_map/pallas_call | solution.py:675
  30.5 1.9 %all-to-all-done.1.sum_ref = bf16[32,8,128]{2,1,0:T(8,128)(2,1)S(1)} async-done(((bf16[32,8,128]{2,1,0:T(8,128)(2,1)}), bf16[32,8,128]{2,1,0:T(8,128)(2,1)S(1)}, u32[]{:S(2)}, u32[]{:S(2)}) %all-to-all-start.1) | async-done | bytes 65568 | tf_op jit(solution)/shard_map/all_to_all | solution.py:647
  32.4 9.1 %shard_map.126 = (f32[8,128]{1,0:T(8,128)}, f32[3,128]{1,0:T(4,128)}) custom-call(bf16[32,8,128]{2,1,0:T(8,128)(2,1)S(1)} %all-to-all-done.1.sum_ref, f32[8,128]{1,0:T(8,128)S(1)} %get-tuple-element.20.charge_ref, bf16[32,24,128]{2,1,0:T(8,128)(2,1)S(1)} %all-to-all-done.recv_ref, f32[48,4096]{1,0:T(8,128)S(1)} %get-tuple-element.21.third_ref, ...), custom_call_target="tpu_custom_call" | custom-call | tf_op jit(solution)/shard_map/pallas_call | solution.py:693
  (1 shorter events, 0.0 us)
Async XLA Ops:
  0.6 24.3 %copy-start = (s32[3,12288]{1,0:T(4,128)S(1)}, s32[3,12288]{1,0:T(4,128)}, u32[]{:S(2)}) copy-start(s32[3,12288]{1,0:T(4,128)} %wave_ref.1) | copy-start | bytes 442372
  2.4 16.6 %all-to-all-start = ((bf16[32,24,128]{2,1,0:T(8,128)(2,1)}), bf16[32,24,128]{2,1,0:T(8,128)(2,1)S(1)}, u32[]{:S(2)}, u32[]{:S(2)}) async-start(bf16[32,24,128]{2,1,0:T(8,128)(2,1)} %shard_map.122), calls=%async_computation | async-start | bytes 393216 | tf_op jit(solution)/shard_map/all_to_all | solution.py:621
  9.7 0.8 %copy-start.1 = (s32[64,128]{1,0:T(8,128)S(1)}, s32[64,128]{1,0:T(8,128)}, u32[]{:S(2)}) copy-start(s32[64,128]{1,0:T(8,128)} %nbr_ref.3) | copy-start | bytes 98308
  10.5 0.8 %copy-start.2 = (bf16[2,128,128]{2,1,0:T(8,128)(2,1)S(1)}, bf16[2,128,128]{2,1,0:T(8,128)(2,1)}, u32[]{:S(2)}) copy-start(bf16[2,128,128]{2,1,0:T(8,128)(2,1)} %w_in_ref.1) | copy-start | bytes 196612
  11.3 0.8 %copy-start.3 = (bf16[2,128,128]{2,1,0:T(8,128)(2,1)S(1)}, bf16[2,128,128]{2,1,0:T(8,128)(2,1)}, u32[]{:S(2)}) copy-start(bf16[2,128,128]{2,1,0:T(8,128)(2,1)} %w_out_ref.1) | copy-start | bytes 196612
  12.2 0.7 %copy-start.4 = (bf16[2,8,128]{2,1,0:T(8,128)(2,1)S(1)}, bf16[2,8,128]{2,1,0:T(8,128)(2,1)}, u32[]{:S(2)}) copy-start(bf16[2,8,128]{2,1,0:T(8,128)(2,1)} %radial_ref.1) | copy-start | bytes 12292
  12.9 0.7 %copy-start.5 = (bf16[128,8]{0,1:T(8,128)(2,1)S(1)}, bf16[128,8]{0,1:T(8,128)(2,1)}, u32[]{:S(2)}) copy-start(bf16[128,8]{0,1:T(8,128)(2,1)} %param.21) | copy-start | bytes 6148
  13.5 0.7 %copy-start.6 = (bf16[2,128]{1,0:T(2,128)(2,1)S(1)}, bf16[2,128]{1,0:T(2,128)(2,1)}, u32[]{:S(2)}) copy-start(bf16[2,128]{1,0:T(2,128)(2,1)} %emb_ref.1) | copy-start | bytes 1540
  14.2 0.7 %copy-start.7 = (bf16[2,128]{1,0:T(2,128)(2,1)S(1)}, bf16[2,128]{1,0:T(2,128)(2,1)}, u32[]{:S(2)}) copy-start(bf16[2,128]{1,0:T(2,128)(2,1)} %gain_ref.1) | copy-start | bytes 1540
  22.2 10.2 %all-to-all-start.1 = ((bf16[32,8,128]{2,1,0:T(8,128)(2,1)}), bf16[32,8,128]{2,1,0:T(8,128)(2,1)S(1)}, u32[]{:S(2)}, u32[]{:S(2)}) async-start(bf16[32,8,128]{2,1,0:T(8,128)(2,1)} %get-tuple-element.19), calls=%async_computation.1 | async-start | bytes 131072 | tf_op jit(solution)/shard_map/all_to_all | solution.py:647
